TPU v7x, 128 devices: a whole 4x4x4 slice. The times are simulated.
128 devices in a mesh: visit: 4 (over x), patch: 32 (over z, y, core).
Axes of the slice: x: 4, y: 4, z: 4, core: 2. Of those that a mesh axis runs over, the one named last changes fastest.
Arguments:
- image: float32 [4096, 128, 128], P(('visit', 'patch')), may hold values from -6 to 6
- variance: float32 [4096, 128, 128], P(('visit', 'patch')), may hold values from 0.25 to 4
- intersections: int32 [4096, 2], P(('visit', 'patch')), may hold values from 0 to 31, all different within a row; in each aligned block of 32 rows (0 to 31, 32 to 63, ...) at most 3 rows name the same one
- boxes: int32 [4096, 2, 2], P(('visit', 'patch')), may hold values from -64 to 191
- shifts: float32 [4096, 2, 2], P(('visit', 'patch')), may hold values from 0 to 1
- basis_ids: int32 [4096, 3], P(('visit', 'patch')), may hold values from 0 to 7
- coefs: float32 [4096, 3], P(('visit', 'patch')), may hold values from 0.3 to 1.5
- taps: float32 [8, 2, 41], replicated, may hold values from -1 to 1
Outputs:
- coadd: float32 [8192, 256], P('patch')
- coadd_var: float32 [8192, 256], P('patch')
Inputs may be any that keep to these rules, and one draw needn't show every extreme that they name: `intersections`: the rows of one device name every patch at most 3 times; each tile names two different patches.
All inputs are finite; a program needn't handle non-finite values.
Results may differ from a plain program's by a relative error of at most 0.0003.
Values sent between devices are 32-bit elements; how exact they have to be, the bound alone decides.
No kernel may reach another device: no remote copies, remote signals or barrier semaphores. Data moves between devices by JAX's collectives and lax.ppermute only.
A program may use at most 128 MiB of HBM per device.

v0:
```python
import functools

import jax
import jax.numpy as jnp
from jax import lax
from jax.experimental import pallas as pl
from jax.experimental.pallas import tpu as pltpu
from jax.sharding import PartitionSpec as P

TS = 128
PATCH = 256
NB = 3
NBASIS = 8
HALF = 20
TILES = 32
ROUTES = 2 * TILES
CAP = 3
META = 24
MAIN = 160
PART = (PATCH - MAIN) // 4
PITCH = TS + 8
PAD = 64
F32 = jnp.float32
BF16 = jnp.bfloat16

EMPTY = 1 << 24
UNROLL = 8
MATCH_UNROLL = 16
CHUNKS = 2
MATCH_COST = 100_000_000_000
WARP_COST = 10_000_000_000


def split(x):
    high = x.astype(BF16)
    return high, (x - high.astype(F32)).astype(BF16)


def here():
    patch = lax.axis_index("patch")
    z, y = patch >> 3, (patch >> 1) & 3
    return z, y, patch & 1, lax.axis_index("visit") * 16 + z * 4 + y


def quarter(first, second, core):
    visit = lax.axis_index("visit")
    edges = jnp.where(core == 0, first + 2 * second, 2 * first + second)
    return (visit ^ (visit >> 1)) ^ edges


def place_code(z, y, core):
    first, second = jnp.where(core == 0, z, y), jnp.where(core == 0, y, z)
    first, second = first ^ (first >> 1), second ^ (second >> 1)
    return ((first & 1) << 3) | ((first >> 1) << 2) | ((second & 1) << 1) | (second >> 1)


def pack_kernel(intersections, boxes, shifts, out):
    z, y, _, _ = here()
    out[...] = jnp.zeros_like(out)
    earlier_item = lax.broadcasted_iota(jnp.int32, (TILES, TILES), 0)
    item = lax.broadcasted_iota(jnp.int32, (TILES, TILES), 1)
    dest = [intersections[route : route + 1, :] for route in range(2)]

    def earlier(rows):
        columns = [jnp.sum(jnp.where(earlier_item == item, row, 0), axis=1, keepdims=True) for row in rows]
        counts = []
        for route, row in enumerate(rows):
            same = jnp.where((columns[route] == row) & (earlier_item < item), 1, 0)
            if route == 1:
                same = same + jnp.where(columns[0] == row, 1, 0)
            counts.append(jnp.sum(same, axis=0, keepdims=True))
        return counts

    slots, places = earlier(dest), earlier([d & 1 for d in dest])
    for route in range(2):
        d = dest[route]
        code = place_code(d >> 3, (d >> 1) & 3, d & 1) ^ place_code(z, y, d & 1)
        out[route : route + 1, 0:TILES] = (code + (slots[route] << 4) + ((d & 1) << 8)).astype(F32)
        out[10 + route : 11 + route, 0:TILES] = places[route].astype(F32)
        out[2 + 2 * route : 4 + 2 * route, 0:TILES] = boxes[route].astype(F32)
        out[6 + 2 * route : 8 + 2 * route, 0:TILES] = shifts[route]
    second = jnp.sum(intersections[...] & 1).astype(F32)
    lane = lax.broadcasted_iota(jnp.int32, (1, TS), 1)
    out[12:13, :] = jnp.where(lane == 0, ROUTES - second, second)


def pack(intersections, boxes, shifts):
    vmem = pl.BlockSpec(memory_space=pltpu.VMEM)
    return pl.pallas_call(
        pack_kernel,
        out_shape=jax.ShapeDtypeStruct((16, TS), F32),
        in_specs=[vmem] * 3,
        out_specs=vmem,
        name="pack",
    )(intersections.T, boxes.transpose(1, 2, 0), shifts.transpose(1, 2, 0))


def match_kernel(
    ids_hbm, coefs_hbm, taps_hbm, image_hbm, out, basis_ids, coefs, taps, line, row_mats, col_mats, image, sems, small_sems
):
    size = TILES // CHUNKS
    copies = [
        pltpu.make_async_copy(image_hbm.at[pl.ds(c * size, size)], image.at[pl.ds(c * size, size)], sems.at[c])
        for c in range(CHUNKS)
    ]
    small = [
        pltpu.make_async_copy(source, target, small_sems.at[i])
        for i, (source, target) in enumerate(((taps_hbm, taps), (ids_hbm, basis_ids), (coefs_hbm, coefs)))
    ]
    for copy in small + copies:
        copy.start()
    i = lax.broadcasted_iota(jnp.int32, (TS, TS), 0)
    k = lax.broadcasted_iota(jnp.int32, (TS, TS), 1)
    near = jnp.abs(i - k) <= HALF
    none = jnp.zeros((TS, TS), BF16)
    line[...] = jnp.zeros_like(line)
    for copy in small:
        copy.wait()
    for b in range(NBASIS):
        line[2 * b : 2 * b + 2, 0 : 2 * HALF + 1] = taps[b]
    line[...] = pltpu.roll(line[...], TS - HALF, 1)

    def square(high, low):
        return jnp.concatenate([jnp.concatenate([high, low], 1), jnp.concatenate([high, none], 1)], 0)

    for b in range(NBASIS):
        for side in range(2):
            band = jnp.broadcast_to(line[2 * b + side : 2 * b + side + 1, :], (TS, TS))
            band = jnp.where(near, pltpu.roll(band, 0, 1, stride=1, stride_axis=0), 0.0)
            if side == 0:
                row_mats[b] = jnp.concatenate(split(band.T), 1)
            else:
                col_mats[b] = square(*split(band))

    out[TILES * PITCH :, :] = jnp.zeros((8, TS), F32)
    for c in range(CHUNKS):
        copies[c].wait()

        @pl.loop(c * size, (c + 1) * size, step=MATCH_UNROLL)
        def _(first):
            for t in [first + u for u in range(MATCH_UNROLL)]:
                pixels = square(*split(image[t]))
                bases = [basis_ids[j, t] for j in range(NB)]
                bands = jnp.concatenate([row_mats[basis] for basis in bases], 0)
                p = jnp.dot(bands, pixels, preferred_element_type=F32)
                p = p[:, :TS] + p[:, TS:]
                parts = [jnp.concatenate(split(p[TS * j : TS * (j + 1)] * coefs[j, t]), 1) for j in range(NB)]
                bands = jnp.concatenate([col_mats[basis] for basis in bases], 0)
                total = jnp.dot(jnp.concatenate(parts, 1), bands, preferred_element_type=F32)
                at = pl.multiple_of(t * PITCH, 8)
                out[pl.ds(at, 8), :] = jnp.zeros((8, TS), F32)
                out[pl.ds(at + 8, TS), :] = total[:, :TS] + total[:, TS:]


def match(basis_ids, coefs, taps, image):
    vmem, hbm = pl.BlockSpec(memory_space=pltpu.VMEM), pl.BlockSpec(memory_space=pltpu.HBM)
    return pl.pallas_call(
        match_kernel,
        out_shape=jax.ShapeDtypeStruct((TILES * PITCH + 8, TS), F32),
        in_specs=[hbm] * 4,
        out_specs=vmem,
        scratch_shapes=[
            pltpu.SMEM((NB, TILES), jnp.int32),
            pltpu.SMEM((NB, TILES), F32),
            pltpu.VMEM((NBASIS, 2, 2 * HALF + 1), F32),
            pltpu.VMEM((2 * NBASIS, TS), F32),
            pltpu.VMEM((NBASIS, TS, 2 * TS), BF16),
            pltpu.VMEM((NBASIS, 2 * TS, 2 * TS), BF16),
            pltpu.VMEM((TILES, TS, TS), F32),
            pltpu.SemaphoreType.DMA((CHUNKS,)),
            pltpu.SemaphoreType.DMA((3,)),
        ],
        compiler_params=pltpu.CompilerParams(vmem_limit_bytes=40 << 20),
        cost_estimate=pl.CostEstimate(flops=MATCH_COST, bytes_accessed=6 << 20, transcendentals=0),
        name="match",
    )(*(pltpu.with_memory_space_constraint(x, pltpu.HBM) for x in (basis_ids.T, coefs.T, taps, image)))


def warp_kernel(with_meta, *refs):
    if with_meta:
        own, other, own_raw, other_raw = refs[:4]
        outs, slots, weights = refs[4:10], refs[10], refs[11]
        acc, meta, own_tiles, other_tiles = refs[12:]
    else:
        slots, own, other, weights, own_tiles, other_tiles = refs[:6]
        outs, acc = refs[6:10], refs[10]
    lane = lax.broadcasted_iota(jnp.int32, (8, TS), 1)
    for k in range(16):
        for side in (1, 2):
            acc[4 * k + side, PAD : PAD + PATCH, :] = jnp.zeros((PATCH, TS), F32)

    if with_meta:
        _, _, core, chip = here()
        meta[...] = jnp.zeros_like(meta)

        @pl.loop(0, TILES, step=8)
        def _(first):
            for side, table, raw, tiles in ((0, own, own_raw, own_tiles), (1, other, other_raw, other_tiles)):
                for route in range(2):
                    for t in [first + u for u in range(8)]:
                        what = table[route, t].astype(jnp.int32)
                        at = jnp.where((what >> 8) == core, table[10 + route, t].astype(jnp.int32) + 1, 127)
                        slots[side, at] = (what << 8) + (2 * t + route)
                sums = []
                for t in [first + u for u in range(8)]:
                    tile = raw[t]
                    at = pl.multiple_of(t * PITCH, 8)
                    tiles[pl.ds(at, 8), :] = jnp.zeros((8, TS), F32)
                    tiles[pl.ds(at + 8, TS), :] = tile
                    sums.append(jnp.sum(tile, axis=0, keepdims=True))
                sums = jnp.sum(jnp.concatenate(sums, 0), axis=1, keepdims=True)
                at = pl.multiple_of(side * TILES + first, 8)
                weights[pl.ds(at, 8), :] = jnp.broadcast_to(float(TS * TS) / sums, (8, TS))

        for side, table in ((0, own), (1, other)):
            n = table[12, core].astype(jnp.int32)
            slots[side, 0] = n
            for u in range(UNROLL):
                slots[side, 1 + n + u] = EMPTY
        for tiles in (own_tiles, other_tiles):
            tiles[TILES * PITCH :, :] = jnp.zeros((8, TS), F32)

    def place(entry, side, table, tiles):
        item, k, slot = entry & 255, (entry >> 8) & 15, (entry >> 12) & 3
        t, route = item >> 1, item & 1
        row, col = table[2 + 2 * route, t].astype(jnp.int32), table[3 + 2 * route, t].astype(jnp.int32)
        frac_row, frac_col = table[6 + 2 * route, t], table[7 + 2 * route, t]
        real = jnp.where(entry >= EMPTY, 0.0, 1.0)
        weight = jnp.broadcast_to(weights[pl.ds(side * TILES + t, 1), :], (8, TS))
        scale = weight * real
        if with_meta:
            field = lax.broadcasted_iota(jnp.int32, (8, TS), 0)
            value = jnp.where(field == 1, row.astype(F32), weight)
            value = jnp.where(field == 2, col.astype(F32), value)
            value = jnp.where(field == 3, frac_row, value)
            value = jnp.where(field == 4, frac_col, value)
            value = jnp.where((field < 5) & (lane == 2 * chip + side), value * real, 0.0)
            meta[k * CAP + slot] += value
            scale = scale * weight
        near, far = scale * (1.0 - frac_col), scale * frac_col
        turn, down = (col + TS) & (TS - 1), (row + PAD) & 7
        here = jnp.where(lane >= turn, near, 0.0)
        here_next = jnp.where(lane >= turn + 1, far, 0.0)
        over, over_next = near - here, far - here_next
        start = t * PITCH + 8 - down
        upper, lower = tiles[pl.ds(start, PITCH), :], tiles[pl.ds(start - 1, PITCH), :]
        rows = upper * (1.0 - frac_row) + lower * frac_row
        r0 = pltpu.roll(rows, turn, 1).reshape(PITCH // 8, 8, TS)
        r1 = pltpu.roll(rows, (turn + 1) & (TS - 1), 1).reshape(PITCH // 8, 8, TS)
        left = (r0 * here + r1 * here_next).reshape(PITCH, TS)
        right = (r0 * over + r1 * over_next).reshape(PITCH, TS)
        return left, right, 4 * k + ((col + TS) >> 7), pl.multiple_of(((row + PAD) >> 3) * 8, 8)

    for side, table, tiles in ((0, own, own_tiles), (1, other, other_tiles)):

        @pl.loop(0, (slots[side, 0] + UNROLL - 1) // UNROLL)
        def _(m, side=side, table=table, tiles=tiles):
            for u in range(UNROLL):
                left, right, first, base = place(slots[side, 1 + m * UNROLL + u], side, table, tiles)
                acc[first, pl.ds(base, PITCH), :] += left
                acc[first + 1, pl.ds(base, PITCH), :] += right

    for k in range(16):
        a, b, c, d = k >> 3, (k >> 2) & 1, (k >> 1) & 1, k & 1
        rest = 2 * c + d if with_meta else 2 * d + c
        rows = MAIN if with_meta else PATCH
        left, right = outs[a], outs[2 + b]
        left[4 * b + rest, 0:rows, :] = acc[4 * k + 1, PAD : PAD + rows, :]
        right[4 * a + rest, :, :] = acc[4 * k + 2, PAD : PAD + rows, :]
        if with_meta:
            for slot in range(CAP):
                left[4 * b + rest, MAIN + 8 * slot : MAIN + 8 * slot + 8, :] = meta[k * CAP + slot]

    if with_meta:
        for first in range(2):
            for second in range(2):
                start = pl.multiple_of(PAD + MAIN + PART * quarter(first, second, core), 8)
                for k in range(16):
                    for half in range(2):
                        part = acc[4 * k + 1 + half, pl.ds(start, PART), :]
                        outs[4 + first][second, k, PART * half : PART * (half + 1), :] = part


def warp(with_meta, *args):
    smem, vmem = pl.BlockSpec(memory_space=pltpu.SMEM), pl.BlockSpec(memory_space=pltpu.VMEM)
    left = jax.ShapeDtypeStruct((8, MAIN + META if with_meta else PATCH, TS), F32)
    right = jax.ShapeDtypeStruct((8, MAIN if with_meta else PATCH, TS), F32)
    outs, specs = [left, left, right, right], [vmem] * 4
    if with_meta:
        outs += [jax.ShapeDtypeStruct((2, 16, 2 * PART, TS), F32)] * 2
        specs += [vmem] * 2
    scratch = [pltpu.VMEM((64, 384, TS), F32)]
    if with_meta:
        outs += [jax.ShapeDtypeStruct((2, 128), jnp.int32), jax.ShapeDtypeStruct((2 * TILES, TS), F32)]
        specs += [smem, vmem]
        scratch += [pltpu.VMEM((16 * CAP, 8, TS), F32)] + [pltpu.VMEM((TILES * PITCH + 8, TS), F32)] * 2
    scalars = 2 if with_meta else 3
    return pl.pallas_call(
        functools.partial(warp_kernel, with_meta),
        out_shape=outs,
        in_specs=[smem] * scalars + [vmem] * (len(args) - scalars),
        out_specs=specs,
        scratch_shapes=scratch,
        compiler_params=pltpu.CompilerParams(vmem_limit_bytes=40 << 20),
        cost_estimate=pl.CostEstimate(flops=WARP_COST, bytes_accessed=8 << 20, transcendentals=0),
        name="warp_meta" if with_meta else "warp",
    )(*args)


def cover_kernel(var, got, coadd_var, safe_ref):
    place_of = lax.broadcasted_iota(jnp.int32, (PATCH, TS), 0).astype(F32)

    def cover(offset, shift):
        u = place_of - offset
        lower = jnp.where((u >= 0.0) & (u <= TS - 1.0), 1.0 - shift, 0.0)
        return lower + jnp.where((u >= 1.0) & (u <= float(TS)), shift, 0.0)

    downs, acrosses = [], []
    for slot in range(CAP):
        at = MAIN + 8 * slot
        fields = var[at : at + 8, :] + got[at : at + 8, :]
        weight, row, col, frac_row, frac_col = (fields[f : f + 1, :] for f in range(5))
        down, down_low = split(cover(row, frac_row) * weight)
        across, across_low = split(cover(col, frac_col))
        downs += [down, down_low, down]
        acrosses += [across, across, across_low]
    den = lax.dot_general(
        jnp.concatenate(downs, 1), jnp.concatenate(acrosses, 1), (((1,), (1,)), ((), ())), preferred_element_type=F32
    )
    safe = jnp.maximum(den, 1.0)
    safe_ref[...] = safe
    for half in range(2):
        lo, lanes = half * (MAIN + META), slice(half * TS, (half + 1) * TS)
        part = safe[0:MAIN, lanes]
        coadd_var[0:MAIN, lanes] = (var[lo : lo + MAIN, :] + got[lo : lo + MAIN, :]) / (part * part)
    core = here()[2]
    for second, source in ((0, var), (1, got)):
        for first in range(2):
            rows = pl.ds(pl.multiple_of(MAIN + PART * quarter(first, second, core), 8), PART)
            for half in range(2):
                lo, lanes = 2 * MAIN + META + PART * (2 * first + half), slice(half * TS, (half + 1) * TS)
                part = safe_ref[rows, lanes]
                coadd_var[rows, lanes] = source[lo : lo + PART, :] / (part * part)


def divide_kernel(num, got, safe, coadd):
    for half in range(2):
        rows, lanes = slice(half * PATCH, (half + 1) * PATCH), slice(half * TS, (half + 1) * TS)
        coadd[:, lanes] = (num[rows, :] + got[rows, :]) / safe[:, lanes]


def finish(kernel, name, outs, *args):
    vmem = pl.BlockSpec(memory_space=pltpu.VMEM)
    return pl.pallas_call(
        kernel,
        out_shape=[jax.ShapeDtypeStruct((PATCH, PATCH), F32)] * outs,
        in_specs=[vmem] * len(args),
        out_specs=[vmem] * outs,
        compiler_params=pltpu.CompilerParams(vmem_limit_bytes=8 << 20),
        cost_estimate=pl.CostEstimate(flops=1_000_000_000, bytes_accessed=1 << 20, transcendentals=0),
        name=name,
    )(*args)


EDGES = (((0, 1), (1, 0), (2, 3), (3, 2)), ((1, 2), (2, 1), (3, 0), (0, 3)))


def over_patch(axis, edge):
    pairs = []
    for a, b in EDGES[edge]:
        for other in range(4):
            for core in range(2):
                src, dst = ((a, other), (b, other)) if axis == core else ((other, a), (other, b))
                pairs.append((src[0] * 8 + src[1] * 2 + core, dst[0] * 8 + dst[1] * 2 + core))
    return pairs


def over_visit(edge):
    return [
        (a * 32 + 2 * chip + core, b * 32 + 2 * chip + core)
        for core in range(2)
        for a, b in EDGES[edge ^ core]
        for chip in range(16)
    ]


def combine(var, num):
    def cross(x, axis, edge):
        return lax.ppermute(x, "patch", over_patch(axis, edge))

    def visit(x, edge):
        return lax.ppermute(x, ("visit", "patch"), over_visit(edge))

    def fold(keep, got):
        n = keep.shape[0] // 2
        return keep[:n] + got[:n], keep[n:] + got[n:]

    def after(got, *earlier):
        return lax.optimization_barrier((*got, *earlier))[: len(got)]

    (vl, vl_send, vr, vr_send, vp, vp_send), (nl, nl_send, nr, nr_send) = var, num
    vl_got, vr_got, vp_got = cross(vl_send, 0, 0), cross(vr_send, 0, 1), visit(vp_send, 0)
    nl_got, nr_got = cross(nl_send, 0, 0), cross(nr_send, 0, 1)

    (vl, vl_send), (vr, vr_send) = fold(vl, vl_got), fold(vr, vr_got)
    vp, vp_send = vp[0] + vp_got[0], vp[1] + vp_got[1]
    vl_got, vr_got, vp_got = cross(vl_send, 0, 1), cross(vr_send, 0, 0), visit(vp_send, 1)
    nl_got, nr_got = after((nl_got, nr_got), vl_send, vr_send, vp_send)
    vp, vp_send = fold(vp, vp_got)
    vp, vp_send = fold(vp, cross(vp_send, 0, 0))
    vp = vp + cross(vp_send, 0, 1)

    (nl, nl_send), (nr, nr_send) = fold(nl, nl_got), fold(nr, nr_got)
    nl_got, nr_got = cross(nl_send, 0, 1), cross(nr_send, 0, 0)

    vl_got, vr_got = after((vl_got, vr_got), nl_send, nr_send, vp_send)
    v, v_send = (
        jnp.concatenate([vl[p] + vl_got[p], vr[p] + vr_got[p], vp[p]], 1) for p in (slice(0, 2), slice(2, 4))
    )
    v_got = cross(v_send, 1, 0)

    nl_got, nr_got = after((nl_got, nr_got), v_send)
    n, n_send = (jnp.concatenate([nl[p] + nl_got[p], nr[p] + nr_got[p]], 1) for p in (slice(0, 2), slice(2, 4)))
    n_got = cross(n_send, 1, 1)

    v, v_send = fold(v, v_got)
    v = v[0] + cross(v_send, 1, 1)[0]
    (n_got,) = after((n_got,), v_send)
    n, n_send = fold(n, n_got)
    n = n[0] + cross(n_send, 1, 0)[0]

    v_got, main = visit(v, 0), 2 * MAIN + META
    v = jnp.concatenate([v[:main] + v_got[:main], v[main:], v_got[main:]], 0)
    n = n + visit(n, 0)
    return (v, visit(v, 1)), (n, visit(n, 1))


def shards(image, variance, intersections, boxes, shifts, basis_ids, coefs, taps):
    swap = [(i, i ^ 1) for i in range(32)]
    other_variance = lax.ppermute(variance, "patch", swap)
    table = pack(intersections, boxes, shifts)
    other_table = lax.ppermute(table, "patch", swap)
    matched = match(basis_ids, coefs, taps, image)
    matched, other_table = lax.optimization_barrier((matched, other_table))
    other_matched = lax.ppermute(matched, "patch", swap)
    *var, slots, weights = warp(True, table, other_table, variance, other_variance)
    num = warp(False, slots, table, other_table, weights, matched, other_matched)
    var, num = combine(var, num)
    coadd_var, safe = finish(cover_kernel, "cover", 2, *var)
    (coadd,) = finish(divide_kernel, "divide", 1, *num, safe)
    return coadd, coadd_var


def solution(mesh):
    split_spec = ("visit", "patch")
    in_specs = (
        P(split_spec, None, None),
        P(split_spec, None, None),
        P(split_spec, None),
        P(split_spec, None, None),
        P(split_spec, None, None),
        P(split_spec, None),
        P(split_spec, None),
        P(),
    )
    out_specs = (P("patch", None), P("patch", None))
    return jax.shard_map(shards, mesh=mesh, in_specs=in_specs, out_specs=out_specs, check_vma=False)
```

profile of v0, /device:TPU:0, one launch (start us, length us, event | category | flops | bytes accessed | tf_op | source)
XLA Modules:
  0.0 91.5 jit_solution(14694635303191029858)
XLA Ops:
  2.6 5.3 %match.1.refs_4_ = f32[4360,128]{1,0:T(8,128)S(1)} custom-call(s32[3,32]{1,0:T(4,128)} %bitcast.28, f32[3,32]{1,0:T(4,128)} %bitcast.29, f32[8,2,41]{2,1,0:T(2,128)} %taps_hbm.1, f32[32,128,128]{2,1,0:T(8,128)} %image_hbm.1), custom_call_target="tpu_custom_call" | custom-call | flops 99999997952 | bytes 6291456 | tf_op jit(solution)/shard_map/match/pallas_call | solution.py:157
  8.1 6.4 %warp_meta.1 = (f32[8,184,128]{2,1,0:T(8,128)S(1)}, f32[8,184,128]{2,1,0:T(8,128)S(1)}, f32[8,160,128]{2,1,0:T(8,128)S(1)}, f32[8,160,128]{2,1,0:T(8,128)S(1)}, ...) custom-call(f32[16,128]{1,0:T(8,128)S(1)} %copy-done, ...), custom_call_target="tpu_custom_call" | custom-call | flops 10000000000 | bytes 8388608 | tf_op jit(solution)/shard_map/warp_meta/pallas_call | solution.py:298
  14.5 4.2 %collective-permute-start.6 = (f32[8,160,128]{2,1,0:T(8,128)S(1)}, f32[8,160,128]{2,1,0:T(8,128)S(1)}, u32[]{:S(2)}, u32[]{:S(2)}) collective-permute-start(f32[8,160,128]{2,1,0:T(8,128)S(1)} %get-tuple-element.35), channel_id=1, source_target_pairs={{8,16},{3,5},{10,18},{11,13},{12,20},{19,21},{14,22},{27,29},{16,8... | collective-permute-start | bytes 1966088 | tf_op jit(solution)/shard_map/ppermute | solution.py:389
  18.7 1.7 %collective-permute-start.7 = (f32[2,16,48,128]{3,2,1,0:T(8,128)S(1)}, f32[2,16,48,128]{3,2,1,0:T(8,128)S(1)}, u32[]{:S(2)}, u32[]{:S(2)}) collective-permute-start(f32[2,16,48,128]{3,2,1,0:T(8,128)S(1)} %get-tuple-element.37), channel_id=1, source_target_pairs={{0,32},{2,34},{4,36},{6,38},{8,40},{10,42},{12,44},{14,46},{16,48}... | collective-permute-start | bytes 2359304 | tf_op jit(solution)/shard_map/ppermute | solution.py:392
  20.4 4.7 %warp.1 = (f32[8,256,128]{2,1,0:T(8,128)S(1)}, f32[8,256,128]{2,1,0:T(8,128)S(1)}, f32[8,256,128]{2,1,0:T(8,128)S(1)}, f32[8,256,128]{2,1,0:T(8,128)S(1)}) custom-call(s32[2,128]{1,0:T(2,128)S(1)} %get-tuple-element.26.refs_0_, f32[16,128]{1,0:T(8,128)S(1)} %copy-done, f32[16,128]{1,0:T(8,128)S(1)} %collective-permute-done.refs_1_.refs_2_, ...), custom_call_target="tpu_custom_call" | custom-call | flops 10000000000 | bytes 8388608 | tf_op jit(solution)/shard_map/warp/pallas_call | solution.py:298
  25.1 1.9 %collective-permute-start.3 = (f32[8,256,128]{2,1,0:T(8,128)S(1)}, f32[8,256,128]{2,1,0:T(8,128)S(1)}, u32[]{:S(2)}, u32[]{:S(2)}) collective-permute-start(f32[8,256,128]{2,1,0:T(8,128)S(1)} %get-tuple-element.30), channel_id=1, source_target_pairs={{0,8},{1,3},{2,10},{9,11},{4,12},{17,19},{6,14},{25,27},{8,0},{3,1... | collective-permute-start | bytes 3145736 | tf_op jit(solution)/shard_map/ppermute | solution.py:389
  27.1 3.6 %collective-permute-done.7 = f32[2,16,48,128]{3,2,1,0:T(8,128)S(1)} collective-permute-done((f32[2,16,48,128]{3,2,1,0:T(8,128)S(1)}, f32[2,16,48,128]{3,2,1,0:T(8,128)S(1)}, u32[]{:S(2)}, u32[]{:S(2)}) %collective-permute-start.7) | collective-permute-done | bytes 786464 | tf_op jit(solution)/shard_map/ppermute | solution.py:392
  30.8 2.8 %collective-permute-start.12 = (f32[16,48,128]{2,1,0:T(8,128)S(1)}, f32[16,48,128]{2,1,0:T(8,128)S(1)}, u32[]{:S(2)}, u32[]{:S(2)}) collective-permute-start(f32[16,48,128]{2,1,0:T(8,128)S(1)} %get-tuple-element.53), channel_id=1, source_target_pairs={{32,64},{34,66},{36,68},{38,70},{40,72},{42,74},{44,76},{46,78},{4... | collective-permute-start | bytes 1179656 | tf_op jit(solution)/shard_map/ppermute | solution.py:392
  33.7 2.1 %collective-permute-start.11 = (f32[4,160,128]{2,1,0:T(8,128)S(1)}, f32[4,160,128]{2,1,0:T(8,128)S(1)}, u32[]{:S(2)}, u32[]{:S(2)}) collective-permute-start(f32[4,160,128]{2,1,0:T(8,128)S(1)} %get-tuple-element.57), channel_id=1, source_target_pairs={{0,8},{1,3},{2,10},{9,11},{4,12},{17,19},{6,14},{25,27},{8,0},{3,1... | collective-permute-start | bytes 983048 | tf_op jit(solution)/shard_map/ppermute | solution.py:389
  36.1 3.7 %collective-permute-done.12 = f32[16,48,128]{2,1,0:T(8,128)S(1)} collective-permute-done((f32[16,48,128]{2,1,0:T(8,128)S(1)}, f32[16,48,128]{2,1,0:T(8,128)S(1)}, u32[]{:S(2)}, u32[]{:S(2)}) %collective-permute-start.12) | collective-permute-done | bytes 393248 | tf_op jit(solution)/shard_map/ppermute | solution.py:392
  39.9 2.1 %collective-permute-start.13 = (f32[8,48,128]{2,1,0:T(8,128)S(1)}, f32[8,48,128]{2,1,0:T(8,128)S(1)}, u32[]{:S(2)}, u32[]{:S(2)}) collective-permute-start(f32[8,48,128]{2,1,0:T(8,128)S(1)} %get-tuple-element.63), channel_id=1, source_target_pairs={{0,8},{1,3},{2,10},{9,11},{4,12},{17,19},{6,14},{25,27},{8,0},{3,1... | collective-permute-start | bytes 589832 | tf_op jit(solution)/shard_map/ppermute | solution.py:389
  43.5 3.7 %collective-permute-done.13 = f32[8,48,128]{2,1,0:T(8,128)S(1)} collective-permute-done((f32[8,48,128]{2,1,0:T(8,128)S(1)}, f32[8,48,128]{2,1,0:T(8,128)S(1)}, u32[]{:S(2)}, u32[]{:S(2)}) %collective-permute-start.13) | collective-permute-done | bytes 196640 | tf_op jit(solution)/shard_map/ppermute | solution.py:389
  47.7 7.2 %collective-permute-done.14 = f32[4,48,128]{2,1,0:T(8,128)S(1)} collective-permute-done((f32[4,48,128]{2,1,0:T(8,128)S(1)}, f32[4,48,128]{2,1,0:T(8,128)S(1)}, u32[]{:S(2)}, u32[]{:S(2)}) %collective-permute-start.14) | collective-permute-done | bytes 98336 | tf_op jit(solution)/shard_map/ppermute | solution.py:389
  54.9 1.6 %collective-permute-start.16 = (f32[2,392,128]{2,1,0:T(8,128)S(1)}, f32[2,392,128]{2,1,0:T(8,128)S(1)}, u32[]{:S(2)}, u32[]{:S(2)}) collective-permute-start(f32[2,392,128]{2,1,0:T(8,128)S(1)} %pad_maximum_fusion.1), channel_id=1, source_target_pairs={{0,2},{1,9},{8,10},{3,11},{16,18},{5,13},{24,26},{7,15},{2,0},{9,1... | collective-permute-start | bytes 1204232 | tf_op jit(solution)/shard_map/ppermute | solution.py:389
  56.7 2.3 %collective-permute-start.15 = (f32[2,512,128]{2,1,0:T(8,128)S(1)}, f32[2,512,128]{2,1,0:T(8,128)S(1)}, u32[]{:S(2)}, u32[]{:S(2)}) collective-permute-start(f32[2,512,128]{2,1,0:T(8,128)S(1)} %pad_maximum_fusion), channel_id=1, source_target_pairs={{2,4},{9,17},{10,12},{11,19},{18,20},{13,21},{26,28},{15,23},{4,2}... | collective-permute-start | bytes 1572872 | tf_op jit(solution)/shard_map/ppermute | solution.py:389
  59.0 3.9 %collective-permute-done.16 = f32[2,392,128]{2,1,0:T(8,128)S(1)} collective-permute-done((f32[2,392,128]{2,1,0:T(8,128)S(1)}, f32[2,392,128]{2,1,0:T(8,128)S(1)}, u32[]{:S(2)}, u32[]{:S(2)}) %collective-permute-start.16) | collective-permute-done | bytes 401440 | tf_op jit(solution)/shard_map/ppermute | solution.py:389
  62.9 3.1 %collective-permute-start.20 = (f32[1,392,128]{2,1,0:T(8,128)S(1)}, f32[1,392,128]{2,1,0:T(8,128)S(1)}, u32[]{:S(2)}, u32[]{:S(2)}) collective-permute-start(f32[1,392,128]{2,1,0:T(8,128)S(1)} %slice_add_fusion.15), channel_id=1, source_target_pairs={{2,4},{9,17},{10,12},{11,19},{18,20},{13,21},{26,28},{15,23},{4,2}... | collective-permute-start | bytes 602120 | tf_op jit(solution)/shard_map/ppermute | solution.py:389
  67.3 2.6 %collective-permute-done.20 = f32[1,392,128]{2,1,0:T(8,128)S(1)} collective-permute-done((f32[1,392,128]{2,1,0:T(8,128)S(1)}, f32[1,392,128]{2,1,0:T(8,128)S(1)}, u32[]{:S(2)}, u32[]{:S(2)}) %collective-permute-start.20) | collective-permute-done | bytes 200736 | tf_op jit(solution)/shard_map/ppermute | solution.py:389
  70.6 3.1 %collective-permute-done.17 = f32[1,512,128]{2,1,0:T(8,128)S(1)} collective-permute-done((f32[1,512,128]{2,1,0:T(8,128)S(1)}, f32[1,512,128]{2,1,0:T(8,128)S(1)}, u32[]{:S(2)}, u32[]{:S(2)}) %collective-permute-start.17) | collective-permute-done | bytes 262176 | tf_op jit(solution)/shard_map/ppermute | solution.py:389
  74.4 1.5 %collective-permute-done.21 = f32[392,128]{1,0:T(8,128)S(1)} collective-permute-done((f32[392,128]{1,0:T(8,128)S(1)}, f32[392,128]{1,0:T(8,128)S(1)}, u32[]{:S(2)}, u32[]{:S(2)}) %collective-permute-start.21) | collective-permute-done | bytes 200736 | tf_op jit(solution)/shard_map/ppermute | solution.py:392
  76.0 3.4 %collective-permute-start.22 = (f32[440,128]{1,0:T(8,128)S(1)}, f32[440,128]{1,0:T(8,128)S(1)}, u32[]{:S(2)}, u32[]{:S(2)}) collective-permute-start(f32[440,128]{1,0:T(8,128)S(1)} %pad_maximum_fusion.4.var), channel_id=1, source_target_pairs={{32,64},{34,66},{36,68},{38,70},{40,72},{42,74},{44,76},{46,78},{4... | collective-permute-start | bytes 675848 | tf_op jit(solution)/shard_map/ppermute | solution.py:392
  79.4 3.6 %collective-permute-done.18 = f32[512,128]{1,0:T(8,128)S(1)} collective-permute-done((f32[512,128]{1,0:T(8,128)S(1)}, f32[512,128]{1,0:T(8,128)S(1)}, u32[]{:S(2)}, u32[]{:S(2)}) %collective-permute-start.18) | collective-permute-done | bytes 262176 | tf_op jit(solution)/shard_map/ppermute | solution.py:392
  83.1 2.2 %collective-permute-start.19 = (f32[512,128]{1,0:T(8,128)S(1)}, f32[512,128]{1,0:T(8,128)S(1)}, u32[]{:S(2)}, u32[]{:S(2)}) collective-permute-start(f32[512,128]{1,0:T(8,128)S(1)} %add.132.num), channel_id=1, source_target_pairs={{32,64},{34,66},{36,68},{38,70},{40,72},{42,74},{44,76},{46,78},{4... | collective-permute-start | bytes 786440 | tf_op jit(solution)/shard_map/ppermute | solution.py:392
  86.5 4.2 %collective-permute-done.19.got = f32[512,128]{1,0:T(8,128)S(1)} collective-permute-done((f32[512,128]{1,0:T(8,128)S(1)}, f32[512,128]{1,0:T(8,128)S(1)}, u32[]{:S(2)}, u32[]{:S(2)}) %collective-permute-start.19) | collective-permute-done | bytes 262176 | tf_op jit(solution)/shard_map/ppermute | solution.py:392
  (56 shorter events, 9.7 us)
Async XLA Ops:
  2.1 5.9 %collective-permute-start = (f32[16,128]{1,0:T(8,128)}, f32[16,128]{1,0:T(8,128)S(1)}, u32[]{:S(2)}, u32[]{:S(2)}) collective-permute-start(f32[16,128]{1,0:T(8,128)} %pack.1.refs_0_.refs_1_), channel_id=1, source_target_pairs={{0,1},{1,0},{2,3},{3,2},{4,5},{5,4},{6,7},{7,6},{8,9},{9,8},{10,11... | collective-permute-start | bytes 24584 | tf_op jit(solution)/shard_map/ppermute | solution.py:442
  2.1 6.0 %collective-permute-start.1 = (f32[32,128,128]{2,1,0:T(8,128)}, f32[32,128,128]{2,1,0:T(8,128)S(1)}, u32[]{:S(2)}, u32[]{:S(2)}) collective-permute-start(f32[32,128,128]{2,1,0:T(8,128)} %refs_2_.1), channel_id=1, source_target_pairs={{0,1},{1,0},{2,3},{3,2},{4,5},{5,4},{6,7},{7,6},{8,9},{9,8},{10,11... | collective-permute-start | bytes 6291464 | tf_op jit(solution)/shard_map/ppermute | solution.py:440
  2.6 5.5 %copy-start.1 = (f32[32,128,128]{2,1,0:T(8,128)S(1)}, f32[32,128,128]{2,1,0:T(8,128)}, u32[]{:S(2)}) copy-start(f32[32,128,128]{2,1,0:T(8,128)} %refs_2_.1) | copy-start | bytes 6291460
  7.9 12.4 %collective-permute-start.2 = (f32[4360,128]{1,0:T(8,128)S(1)}, f32[4360,128]{1,0:T(8,128)S(1)}, u32[]{:S(2)}, u32[]{:S(2)}) collective-permute-start(f32[4360,128]{1,0:T(8,128)S(1)} %match.1.refs_4_), channel_id=1, source_target_pairs={{0,1},{1,0},{2,3},{3,2},{4,5},{5,4},{6,7},{7,6},{8,9},{9,8},{10,11... | collective-permute-start | bytes 6696968 | tf_op jit(solution)/shard_map/ppermute | solution.py:445
  14.5 19.1 %collective-permute-start.6 = (f32[8,160,128]{2,1,0:T(8,128)S(1)}, f32[8,160,128]{2,1,0:T(8,128)S(1)}, u32[]{:S(2)}, u32[]{:S(2)}) collective-permute-start(f32[8,160,128]{2,1,0:T(8,128)S(1)} %get-tuple-element.35), channel_id=1, source_target_pairs={{8,16},{3,5},{10,18},{11,13},{12,20},{19,21},{14,22},{27,29},{16,8... | collective-permute-start | bytes 1966088 | tf_op jit(solution)/shard_map/ppermute | solution.py:389
  18.7 17.1 %collective-permute-start.5 = (f32[8,184,128]{2,1,0:T(8,128)S(1)}, f32[8,184,128]{2,1,0:T(8,128)S(1)}, u32[]{:S(2)}, u32[]{:S(2)}) collective-permute-start(f32[8,184,128]{2,1,0:T(8,128)S(1)} %get-tuple-element.33), channel_id=1, source_target_pairs={{0,8},{1,3},{2,10},{9,11},{4,12},{17,19},{6,14},{25,27},{8,0},{3,1... | collective-permute-start | bytes 2261000 | tf_op jit(solution)/shard_map/ppermute | solution.py:389
  18.7 12.0 %collective-permute-start.7 = (f32[2,16,48,128]{3,2,1,0:T(8,128)S(1)}, f32[2,16,48,128]{3,2,1,0:T(8,128)S(1)}, u32[]{:S(2)}, u32[]{:S(2)}) collective-permute-start(f32[2,16,48,128]{3,2,1,0:T(8,128)S(1)} %get-tuple-element.37), channel_id=1, source_target_pairs={{0,32},{2,34},{4,36},{6,38},{8,40},{10,42},{12,44},{14,46},{16,48}... | collective-permute-start | bytes 2359304 | tf_op jit(solution)/shard_map/ppermute | solution.py:392
  25.1 16.9 %collective-permute-start.3 = (f32[8,256,128]{2,1,0:T(8,128)S(1)}, f32[8,256,128]{2,1,0:T(8,128)S(1)}, u32[]{:S(2)}, u32[]{:S(2)}) collective-permute-start(f32[8,256,128]{2,1,0:T(8,128)S(1)} %get-tuple-element.30), channel_id=1, source_target_pairs={{0,8},{1,3},{2,10},{9,11},{4,12},{17,19},{6,14},{25,27},{8,0},{3,1... | collective-permute-start | bytes 3145736 | tf_op jit(solution)/shard_map/ppermute | solution.py:389
  27.0 16.0 %collective-permute-start.4 = (f32[8,256,128]{2,1,0:T(8,128)S(1)}, f32[8,256,128]{2,1,0:T(8,128)S(1)}, u32[]{:S(2)}, u32[]{:S(2)}) collective-permute-start(f32[8,256,128]{2,1,0:T(8,128)S(1)} %get-tuple-element.31), channel_id=1, source_target_pairs={{8,16},{3,5},{10,18},{11,13},{12,20},{19,21},{14,22},{27,29},{16,8... | collective-permute-start | bytes 3145736 | tf_op jit(solution)/shard_map/ppermute | solution.py:389
  30.8 9.1 %collective-permute-start.12 = (f32[16,48,128]{2,1,0:T(8,128)S(1)}, f32[16,48,128]{2,1,0:T(8,128)S(1)}, u32[]{:S(2)}, u32[]{:S(2)}) collective-permute-start(f32[16,48,128]{2,1,0:T(8,128)S(1)} %get-tuple-element.53), channel_id=1, source_target_pairs={{32,64},{34,66},{36,68},{38,70},{40,72},{42,74},{44,76},{46,78},{4... | collective-permute-start | bytes 1179656 | tf_op jit(solution)/shard_map/ppermute | solution.py:392
  33.7 13.9 %collective-permute-start.11 = (f32[4,160,128]{2,1,0:T(8,128)S(1)}, f32[4,160,128]{2,1,0:T(8,128)S(1)}, u32[]{:S(2)}, u32[]{:S(2)}) collective-permute-start(f32[4,160,128]{2,1,0:T(8,128)S(1)} %get-tuple-element.57), channel_id=1, source_target_pairs={{0,8},{1,3},{2,10},{9,11},{4,12},{17,19},{6,14},{25,27},{8,0},{3,1... | collective-permute-start | bytes 983048 | tf_op jit(solution)/shard_map/ppermute | solution.py:389
  35.9 11.6 %collective-permute-start.10 = (f32[4,184,128]{2,1,0:T(8,128)S(1)}, f32[4,184,128]{2,1,0:T(8,128)S(1)}, u32[]{:S(2)}, u32[]{:S(2)}) collective-permute-start(f32[4,184,128]{2,1,0:T(8,128)S(1)} %get-tuple-element.55), channel_id=1, source_target_pairs={{8,16},{3,5},{10,18},{11,13},{12,20},{19,21},{14,22},{27,29},{16,8... | collective-permute-start | bytes 1130504 | tf_op jit(solution)/shard_map/ppermute | solution.py:389
  39.9 7.3 %collective-permute-start.13 = (f32[8,48,128]{2,1,0:T(8,128)S(1)}, f32[8,48,128]{2,1,0:T(8,128)S(1)}, u32[]{:S(2)}, u32[]{:S(2)}) collective-permute-start(f32[8,48,128]{2,1,0:T(8,128)S(1)} %get-tuple-element.63), channel_id=1, source_target_pairs={{0,8},{1,3},{2,10},{9,11},{4,12},{17,19},{6,14},{25,27},{8,0},{3,1... | collective-permute-start | bytes 589832 | tf_op jit(solution)/shard_map/ppermute | solution.py:389
  43.1 13.4 %collective-permute-start.9 = (f32[4,256,128]{2,1,0:T(8,128)S(1)}, f32[4,256,128]{2,1,0:T(8,128)S(1)}, u32[]{:S(2)}, u32[]{:S(2)}) collective-permute-start(f32[4,256,128]{2,1,0:T(8,128)S(1)} %get-tuple-element.50), channel_id=1, source_target_pairs={{0,8},{1,3},{2,10},{9,11},{4,12},{17,19},{6,14},{25,27},{8,0},{3,1... | collective-permute-start | bytes 1572872 | tf_op jit(solution)/shard_map/ppermute | solution.py:389
  43.3 13.2 %collective-permute-start.8 = (f32[4,256,128]{2,1,0:T(8,128)S(1)}, f32[4,256,128]{2,1,0:T(8,128)S(1)}, u32[]{:S(2)}, u32[]{:S(2)}) collective-permute-start(f32[4,256,128]{2,1,0:T(8,128)S(1)} %get-tuple-element.49), channel_id=1, source_target_pairs={{8,16},{3,5},{10,18},{11,13},{12,20},{19,21},{14,22},{27,29},{16,8... | collective-permute-start | bytes 1572872 | tf_op jit(solution)/shard_map/ppermute | solution.py:389
  47.2 7.7 %collective-permute-start.14 = (f32[4,48,128]{2,1,0:T(8,128)S(1)}, f32[4,48,128]{2,1,0:T(8,128)S(1)}, u32[]{:S(2)}, u32[]{:S(2)}) collective-permute-start(f32[4,48,128]{2,1,0:T(8,128)S(1)} %slice_add_fusion.24), channel_id=1, source_target_pairs={{8,16},{3,5},{10,18},{11,13},{12,20},{19,21},{14,22},{27,29},{16,8... | collective-permute-start | bytes 294920 | tf_op jit(solution)/shard_map/ppermute | solution.py:389
  54.9 7.9 %collective-permute-start.16 = (f32[2,392,128]{2,1,0:T(8,128)S(1)}, f32[2,392,128]{2,1,0:T(8,128)S(1)}, u32[]{:S(2)}, u32[]{:S(2)}) collective-permute-start(f32[2,392,128]{2,1,0:T(8,128)S(1)} %pad_maximum_fusion.1), channel_id=1, source_target_pairs={{0,2},{1,9},{8,10},{3,11},{16,18},{5,13},{24,26},{7,15},{2,0},{9,1... | collective-permute-start | bytes 1204232 | tf_op jit(solution)/shard_map/ppermute | solution.py:389
  56.7 10.5 %collective-permute-start.15 = (f32[2,512,128]{2,1,0:T(8,128)S(1)}, f32[2,512,128]{2,1,0:T(8,128)S(1)}, u32[]{:S(2)}, u32[]{:S(2)}) collective-permute-start(f32[2,512,128]{2,1,0:T(8,128)S(1)} %pad_maximum_fusion), channel_id=1, source_target_pairs={{2,4},{9,17},{10,12},{11,19},{18,20},{13,21},{26,28},{15,23},{4,2}... | collective-permute-start | bytes 1572872 | tf_op jit(solution)/shard_map/ppermute | solution.py:389
  62.9 7.0 %collective-permute-start.20 = (f32[1,392,128]{2,1,0:T(8,128)S(1)}, f32[1,392,128]{2,1,0:T(8,128)S(1)}, u32[]{:S(2)}, u32[]{:S(2)}) collective-permute-start(f32[1,392,128]{2,1,0:T(8,128)S(1)} %slice_add_fusion.15), channel_id=1, source_target_pairs={{2,4},{9,17},{10,12},{11,19},{18,20},{13,21},{26,28},{15,23},{4,2}... | collective-permute-start | bytes 602120 | tf_op jit(solution)/shard_map/ppermute | solution.py:389
  67.2 6.5 %collective-permute-start.17 = (f32[1,512,128]{2,1,0:T(8,128)S(1)}, f32[1,512,128]{2,1,0:T(8,128)S(1)}, u32[]{:S(2)}, u32[]{:S(2)}) collective-permute-start(f32[1,512,128]{2,1,0:T(8,128)S(1)} %fusion.5), channel_id=1, source_target_pairs={{0,2},{1,9},{8,10},{3,11},{16,18},{5,13},{24,26},{7,15},{2,0},{9,1... | collective-permute-start | bytes 786440 | tf_op jit(solution)/shard_map/ppermute | solution.py:389
  69.9 6.0 %collective-permute-start.21 = (f32[392,128]{1,0:T(8,128)S(1)}, f32[392,128]{1,0:T(8,128)S(1)}, u32[]{:S(2)}, u32[]{:S(2)}) collective-permute-start(f32[392,128]{1,0:T(8,128)S(1)} %bitcast.24), channel_id=1, source_target_pairs={{0,32},{2,34},{4,36},{6,38},{8,40},{10,42},{12,44},{14,46},{16,48}... | collective-permute-start | bytes 602120 | tf_op jit(solution)/shard_map/ppermute | solution.py:392
  73.7 9.3 %collective-permute-start.18 = (f32[512,128]{1,0:T(8,128)S(1)}, f32[512,128]{1,0:T(8,128)S(1)}, u32[]{:S(2)}, u32[]{:S(2)}) collective-permute-start(f32[512,128]{1,0:T(8,128)S(1)} %fusion.4), channel_id=1, source_target_pairs={{0,32},{2,34},{4,36},{6,38},{8,40},{10,42},{12,44},{14,46},{16,48}... | collective-permute-start | bytes 786440 | tf_op jit(solution)/shard_map/ppermute | solution.py:392
  76.0 9.3 %collective-permute-start.22 = (f32[440,128]{1,0:T(8,128)S(1)}, f32[440,128]{1,0:T(8,128)S(1)}, u32[]{:S(2)}, u32[]{:S(2)}) collective-permute-start(f32[440,128]{1,0:T(8,128)S(1)} %pad_maximum_fusion.4.var), channel_id=1, source_target_pairs={{32,64},{34,66},{36,68},{38,70},{40,72},{42,74},{44,76},{46,78},{4... | collective-permute-start | bytes 675848 | tf_op jit(solution)/shard_map/ppermute | solution.py:392
  83.1 7.7 %collective-permute-start.19 = (f32[512,128]{1,0:T(8,128)S(1)}, f32[512,128]{1,0:T(8,128)S(1)}, u32[]{:S(2)}, u32[]{:S(2)}) collective-permute-start(f32[512,128]{1,0:T(8,128)S(1)} %add.132.num), channel_id=1, source_target_pairs={{32,64},{34,66},{36,68},{38,70},{40,72},{42,74},{44,76},{46,78},{4... | collective-permute-start | bytes 786440 | tf_op jit(solution)/shard_map/ppermute | solution.py:392
  (1 other events, 5.5 us)
where the time goes:
time: 93.1 us; the launch traced here: 91.5 us
  waiting for transfers between devices  39.4 us (42%)
  starting transfers between devices  30.3 us (33%)
  Pallas kernels  19.9 us (21%)
  other arithmetic  1.13 us (1%)
    ppermute x14, waiting for transfers between devices, cross(): return lax.ppermute(x, 'patch', over_patch(axis, edge))  22.6 us
    ppermute x14, starting transfers between devices, cross(): return lax.ppermute(x, 'patch', over_patch(axis, edge))  18.2 us
    ppermute x6, waiting for transfers between devices, visit(): return lax.ppermute(x, ('visit', 'patch'), over_visit(edge))  16.7 us
    ppermute x6, starting transfers between devices, visit(): return lax.ppermute(x, ('visit', 'patch'), over_visit(edge))  11.4 us
    pallas_call x2, Pallas kernels, warp(): pl.pallas_call(functools.partial(warp_kernel, with_meta), out_shape=outs,...  11.1 us
    pallas_call x1, Pallas kernels, match(): pl.pallas_call(match_kernel, out_shape=jax.ShapeDtypeStruct((TILES * PITC...  5.34 us
    pallas_call x2, Pallas kernels, finish(): pl.pallas_call(kernel, out_shape=[jax.ShapeDtypeStruct((PATCH, PATCH), F3...  2.02 us
  transfers between devices with their start and end apart: 23, of which 12 were waited for; matrix products, arithmetic and copies ran while one was open for 1% of the time, Pallas kernels for 19%

commit v1 on v0

--- a/solution.py
+++ b/solution.py
@@ -334,11 +334,11 @@
         part = safe[0:MAIN, lanes]
         coadd_var[0:MAIN, lanes] = (var[lo : lo + MAIN, :] + got[lo : lo + MAIN, :]) / (part * part)
     core = here()[2]
-    for second, source in ((0, var), (1, got)):
-        for first in range(2):
+    for first, source in ((0, var), (1, got)):
+        for second in range(2):
             rows = pl.ds(pl.multiple_of(MAIN + PART * quarter(first, second, core), 8), PART)
             for half in range(2):
-                lo, lanes = 2 * MAIN + META + PART * (2 * first + half), slice(half * TS, (half + 1) * TS)
+                lo, lanes = 2 * MAIN + META + PART * (2 * second + half), slice(half * TS, (half + 1) * TS)
                 part = safe_ref[rows, lanes]
                 coadd_var[rows, lanes] = source[lo : lo + PART, :] / (part * part)
 
@@ -419,20 +419,21 @@
     )
     v_got = cross(v_send, 1, 0)
 
-    nl_got, nr_got = after((nl_got, nr_got), v_send)
+    nl_got, nr_got = after((nl_got, nr_got), vp_send)
     n, n_send = (jnp.concatenate([nl[p] + nl_got[p], nr[p] + nr_got[p]], 1) for p in (slice(0, 2), slice(2, 4)))
     n_got = cross(n_send, 1, 1)
 
-    v, v_send = fold(v, v_got)
-    v = v[0] + cross(v_send, 1, 1)[0]
     (n_got,) = after((n_got,), v_send)
     n, n_send = fold(n, n_got)
+    (v_got,) = after((v_got,), n_send)
+    v, v_send = fold(v, v_got)
     n = n[0] + cross(n_send, 1, 0)[0]
-
-    v_got, main = visit(v, 0), 2 * MAIN + META
+    v = v[0] + cross(v_send, 1, 1)[0]
+
+    n = n + visit(n, 0)
+    v_got, main = visit(v, 1), 2 * MAIN + META
     v = jnp.concatenate([v[:main] + v_got[:main], v[main:], v_got[main:]], 0)
-    n = n + visit(n, 0)
-    return (v, visit(v, 1)), (n, visit(n, 1))
+    return (v, visit(v, 0)), (n, visit(n, 1))
 
 
 def shards(image, variance, intersections, boxes, shifts, basis_ids, coefs, taps):

time: 93.1 us -> 94.1 us (1.011); the launches traced: 91.5 us -> 93.9 us
  waiting for transfers between devices: 39.4 us -> 41.5 us
  Pallas kernels: 19.9 us -> 21.5 us
  starting transfers between devices: 30.3 us -> 28.9 us
    ppermute x6, starting transfers between devices: 11.4 us -> 9.81 us  [visit(): return lax.ppermute(x, ('visit', 'patch'), over_visit(edge))]
    pallas_call x2, Pallas kernels: 11.1 us -> 12.7 us  [warp(): pl.pallas_call(functools.partial(warp_kernel, with_meta), out_shape=outs,...]
    ppermute x14, waiting for transfers between devices: 22.6 us -> 23.8 us  [cross(): return lax.ppermute(x, 'patch', over_patch(axis, edge))]
    ppermute x6, waiting for transfers between devices: 16.7 us -> 17.8 us  [visit(): return lax.ppermute(x, ('visit', 'patch'), over_visit(edge))]
  transfers between devices with their start and end apart: 23 -> 23, of which waited for: 12 -> 14; matrix products, arithmetic and copies ran while one was open for 1% -> 1% of each run, Pallas kernels for 19% -> 21%
where the time goes in v1:
time: 94.1 us; the launch traced here: 93.9 us
  waiting for transfers between devices  41.5 us (44%)
  starting transfers between devices  28.9 us (31%)
  Pallas kernels  21.5 us (23%)
  other arithmetic  1.09 us (1%)
    ppermute x14, waiting for transfers between devices, cross(): return lax.ppermute(x, 'patch', over_patch(axis, edge))  23.8 us
    ppermute x14, starting transfers between devices, cross(): return lax.ppermute(x, 'patch', over_patch(axis, edge))  18.5 us
    ppermute x6, waiting for transfers between devices, visit(): return lax.ppermute(x, ('visit', 'patch'), over_visit(edge))  17.8 us
    pallas_call x2, Pallas kernels, warp(): pl.pallas_call(functools.partial(warp_kernel, with_meta), out_shape=outs,...  12.7 us
    ppermute x6, starting transfers between devices, visit(): return lax.ppermute(x, ('visit', 'patch'), over_visit(edge))  9.81 us
    pallas_call x1, Pallas kernels, match(): pl.pallas_call(match_kernel, out_shape=jax.ShapeDtypeStruct((TILES * PITC...  5.34 us
    pallas_call x2, Pallas kernels, finish(): pl.pallas_call(kernel, out_shape=[jax.ShapeDtypeStruct((PATCH, PATCH), F3...  2.01 us
  transfers between devices with their start and end apart: 23, of which 14 were waited for; matrix products, arithmetic and copies ran while one was open for 1% of the time, Pallas kernels for 21%

profile of v1, /device:TPU:0, one launch (start us, length us, event | category | flops | bytes accessed | tf_op | source)
XLA Modules:
  0.0 93.9 jit_solution(13358286881461391183)
XLA Ops:
  0.6 1.4 %pack.1.refs_0_.refs_1_ = f32[16,128]{1,0:T(8,128)} custom-call(s32[2,32]{1,0:T(2,128)} %bitcast.27, s32[2,2,32]{2,1,0:T(2,128)} %bitcast.25, f32[2,2,32]{2,1,0:T(2,128)} %bitcast.26), custom_call_target="tpu_custom_call" | custom-call | tf_op jit(solution)/shard_map/pack/pallas_call | solution.py:89
  2.6 5.3 %match.1.refs_4_ = f32[4360,128]{1,0:T(8,128)S(1)} custom-call(s32[3,32]{1,0:T(4,128)} %bitcast.28, f32[3,32]{1,0:T(4,128)} %bitcast.29, f32[8,2,41]{2,1,0:T(2,128)} %taps_hbm.1, f32[32,128,128]{2,1,0:T(8,128)} %image_hbm.1), custom_call_target="tpu_custom_call" | custom-call | flops 99999997952 | bytes 6291456 | tf_op jit(solution)/shard_map/match/pallas_call | solution.py:157
  8.1 7.2 %warp_meta.1 = (f32[8,184,128]{2,1,0:T(8,128)S(1)}, f32[8,184,128]{2,1,0:T(8,128)S(1)}, f32[8,160,128]{2,1,0:T(8,128)S(1)}, f32[8,160,128]{2,1,0:T(8,128)S(1)}, ...) custom-call(f32[16,128]{1,0:T(8,128)S(1)} %copy-done, ...), custom_call_target="tpu_custom_call" | custom-call | flops 10000000000 | bytes 8388608 | tf_op jit(solution)/shard_map/warp_meta/pallas_call | solution.py:298
  15.3 4.2 %collective-permute-start.6 = (f32[8,160,128]{2,1,0:T(8,128)S(1)}, f32[8,160,128]{2,1,0:T(8,128)S(1)}, u32[]{:S(2)}, u32[]{:S(2)}) collective-permute-start(f32[8,160,128]{2,1,0:T(8,128)S(1)} %get-tuple-element.36), channel_id=1, source_target_pairs={{8,16},{3,5},{10,18},{11,13},{12,20},{19,21},{14,22},{27,29},{16,8... | collective-permute-start | bytes 1966088 | tf_op jit(solution)/shard_map/ppermute | solution.py:389
  19.5 1.5 %collective-permute-start.7 = (f32[2,16,48,128]{3,2,1,0:T(8,128)S(1)}, f32[2,16,48,128]{3,2,1,0:T(8,128)S(1)}, u32[]{:S(2)}, u32[]{:S(2)}) collective-permute-start(f32[2,16,48,128]{3,2,1,0:T(8,128)S(1)} %get-tuple-element.38), channel_id=1, source_target_pairs={{0,32},{2,34},{4,36},{6,38},{8,40},{10,42},{12,44},{14,46},{16,48}... | collective-permute-start | bytes 2359304 | tf_op jit(solution)/shard_map/ppermute | solution.py:392
  21.0 5.6 %warp.1 = (f32[8,256,128]{2,1,0:T(8,128)S(1)}, f32[8,256,128]{2,1,0:T(8,128)S(1)}, f32[8,256,128]{2,1,0:T(8,128)S(1)}, f32[8,256,128]{2,1,0:T(8,128)S(1)}) custom-call(s32[2,128]{1,0:T(2,128)S(1)} %get-tuple-element.27.refs_0_, f32[16,128]{1,0:T(8,128)S(1)} %copy-done, f32[16,128]{1,0:T(8,128)S(1)} %collective-permute-done.refs_1_.refs_2_, ...), custom_call_target="tpu_custom_call" | custom-call | flops 10000000000 | bytes 8388608 | tf_op jit(solution)/shard_map/warp/pallas_call | solution.py:298
  26.5 2.1 %collective-permute-start.3 = (f32[8,256,128]{2,1,0:T(8,128)S(1)}, f32[8,256,128]{2,1,0:T(8,128)S(1)}, u32[]{:S(2)}, u32[]{:S(2)}) collective-permute-start(f32[8,256,128]{2,1,0:T(8,128)S(1)} %get-tuple-element.31), channel_id=1, source_target_pairs={{0,8},{1,3},{2,10},{9,11},{4,12},{17,19},{6,14},{25,27},{8,0},{3,1... | collective-permute-start | bytes 3145736 | tf_op jit(solution)/shard_map/ppermute | solution.py:389
  28.7 2.7 %collective-permute-done.7 = f32[2,16,48,128]{3,2,1,0:T(8,128)S(1)} collective-permute-done((f32[2,16,48,128]{3,2,1,0:T(8,128)S(1)}, f32[2,16,48,128]{3,2,1,0:T(8,128)S(1)}, u32[]{:S(2)}, u32[]{:S(2)}) %collective-permute-start.7) | collective-permute-done | bytes 786464 | tf_op jit(solution)/shard_map/ppermute | solution.py:392
  31.6 2.8 %collective-permute-start.10 = (f32[16,48,128]{2,1,0:T(8,128)S(1)}, f32[16,48,128]{2,1,0:T(8,128)S(1)}, u32[]{:S(2)}, u32[]{:S(2)}) collective-permute-start(f32[16,48,128]{2,1,0:T(8,128)S(1)} %get-tuple-element.55), channel_id=1, source_target_pairs={{32,64},{34,66},{36,68},{38,70},{40,72},{42,74},{44,76},{46,78},{4... | collective-permute-start | bytes 1179656 | tf_op jit(solution)/shard_map/ppermute | solution.py:392
  34.5 2.1 %collective-permute-start.14 = (f32[4,160,128]{2,1,0:T(8,128)S(1)}, f32[4,160,128]{2,1,0:T(8,128)S(1)}, u32[]{:S(2)}, u32[]{:S(2)}) collective-permute-start(f32[4,160,128]{2,1,0:T(8,128)S(1)} %get-tuple-element.59), channel_id=1, source_target_pairs={{0,8},{1,3},{2,10},{9,11},{4,12},{17,19},{6,14},{25,27},{8,0},{3,1... | collective-permute-start | bytes 983048 | tf_op jit(solution)/shard_map/ppermute | solution.py:389
  36.9 3.7 %collective-permute-done.10 = f32[16,48,128]{2,1,0:T(8,128)S(1)} collective-permute-done((f32[16,48,128]{2,1,0:T(8,128)S(1)}, f32[16,48,128]{2,1,0:T(8,128)S(1)}, u32[]{:S(2)}, u32[]{:S(2)}) %collective-permute-start.10) | collective-permute-done | bytes 393248 | tf_op jit(solution)/shard_map/ppermute | solution.py:392
  40.7 2.1 %collective-permute-start.11 = (f32[8,48,128]{2,1,0:T(8,128)S(1)}, f32[8,48,128]{2,1,0:T(8,128)S(1)}, u32[]{:S(2)}, u32[]{:S(2)}) collective-permute-start(f32[8,48,128]{2,1,0:T(8,128)S(1)} %get-tuple-element.65), channel_id=1, source_target_pairs={{0,8},{1,3},{2,10},{9,11},{4,12},{17,19},{6,14},{25,27},{8,0},{3,1... | collective-permute-start | bytes 589832 | tf_op jit(solution)/shard_map/ppermute | solution.py:389
  42.8 1.8 %collective-permute-done.4 = f32[8,256,128]{2,1,0:T(8,128)S(1)} collective-permute-done((f32[8,256,128]{2,1,0:T(8,128)S(1)}, f32[8,256,128]{2,1,0:T(8,128)S(1)}, u32[]{:S(2)}, u32[]{:S(2)}) %collective-permute-start.4) | collective-permute-done | bytes 1048608 | tf_op jit(solution)/shard_map/ppermute | solution.py:389
  45.1 2.8 %collective-permute-done.11 = f32[8,48,128]{2,1,0:T(8,128)S(1)} collective-permute-done((f32[8,48,128]{2,1,0:T(8,128)S(1)}, f32[8,48,128]{2,1,0:T(8,128)S(1)}, u32[]{:S(2)}, u32[]{:S(2)}) %collective-permute-start.11) | collective-permute-done | bytes 196640 | tf_op jit(solution)/shard_map/ppermute | solution.py:389
  48.8 5.2 %collective-permute-done.9 = f32[4,256,128]{2,1,0:T(8,128)S(1)} collective-permute-done((f32[4,256,128]{2,1,0:T(8,128)S(1)}, f32[4,256,128]{2,1,0:T(8,128)S(1)}, u32[]{:S(2)}, u32[]{:S(2)}) %collective-permute-start.9) | collective-permute-done | bytes 524320 | tf_op jit(solution)/shard_map/ppermute | solution.py:389
  55.6 4.3 %collective-permute-start.12 = (f32[2,512,128]{2,1,0:T(8,128)S(1)}, f32[2,512,128]{2,1,0:T(8,128)S(1)}, u32[]{:S(2)}, u32[]{:S(2)}) collective-permute-start(f32[2,512,128]{2,1,0:T(8,128)S(1)} %pad_maximum_fusion), channel_id=1, source_target_pairs={{2,4},{9,17},{10,12},{11,19},{18,20},{13,21},{26,28},{15,23},{4,2}... | collective-permute-start | bytes 1572872 | tf_op jit(solution)/shard_map/ppermute | solution.py:389
  60.1 7.0 %collective-permute-done.12 = f32[2,512,128]{2,1,0:T(8,128)S(1)} collective-permute-done((f32[2,512,128]{2,1,0:T(8,128)S(1)}, f32[2,512,128]{2,1,0:T(8,128)S(1)}, u32[]{:S(2)}, u32[]{:S(2)}) %collective-permute-start.12) | collective-permute-done | bytes 524320 | tf_op jit(solution)/shard_map/ppermute | solution.py:389
  67.9 2.5 %collective-permute-start.20 = (f32[1,392,128]{2,1,0:T(8,128)S(1)}, f32[1,392,128]{2,1,0:T(8,128)S(1)}, u32[]{:S(2)}, u32[]{:S(2)}) collective-permute-start(f32[1,392,128]{2,1,0:T(8,128)S(1)} %slice_add_fusion.14), channel_id=1, source_target_pairs={{2,4},{9,17},{10,12},{11,19},{18,20},{13,21},{26,28},{15,23},{4,2}... | collective-permute-start | bytes 602120 | tf_op jit(solution)/shard_map/ppermute | solution.py:389
  70.4 4.5 %collective-permute-done.20 = f32[1,392,128]{2,1,0:T(8,128)S(1)} collective-permute-done((f32[1,392,128]{2,1,0:T(8,128)S(1)}, f32[1,392,128]{2,1,0:T(8,128)S(1)}, u32[]{:S(2)}, u32[]{:S(2)}) %collective-permute-start.20) | collective-permute-done | bytes 200736 | tf_op jit(solution)/shard_map/ppermute | solution.py:389
  75.0 2.2 %collective-permute-start.21 = (f32[392,128]{1,0:T(8,128)S(1)}, f32[392,128]{1,0:T(8,128)S(1)}, u32[]{:S(2)}, u32[]{:S(2)}) collective-permute-start(f32[392,128]{1,0:T(8,128)S(1)} %bitcast.24), channel_id=1, source_target_pairs={{32,64},{34,66},{36,68},{38,70},{40,72},{42,74},{44,76},{46,78},{4... | collective-permute-start | bytes 602120 | tf_op jit(solution)/shard_map/ppermute | solution.py:392
  78.2 4.0 %collective-permute-done.21 = f32[392,128]{1,0:T(8,128)S(1)} collective-permute-done((f32[392,128]{1,0:T(8,128)S(1)}, f32[392,128]{1,0:T(8,128)S(1)}, u32[]{:S(2)}, u32[]{:S(2)}) %collective-permute-start.21) | collective-permute-done | bytes 200736 | tf_op jit(solution)/shard_map/ppermute | solution.py:392
  82.4 3.1 %collective-permute-done.17 = f32[512,128]{1,0:T(8,128)S(1)} collective-permute-done((f32[512,128]{1,0:T(8,128)S(1)}, f32[512,128]{1,0:T(8,128)S(1)}, u32[]{:S(2)}, u32[]{:S(2)}) %collective-permute-start.17) | collective-permute-done | bytes 262176 | tf_op jit(solution)/shard_map/ppermute | solution.py:392
  85.5 2.3 %collective-permute-start.18 = (f32[512,128]{1,0:T(8,128)S(1)}, f32[512,128]{1,0:T(8,128)S(1)}, u32[]{:S(2)}, u32[]{:S(2)}) collective-permute-start(f32[512,128]{1,0:T(8,128)S(1)} %add.129.num), channel_id=1, source_target_pairs={{32,64},{34,66},{36,68},{38,70},{40,72},{42,74},{44,76},{46,78},{4... | collective-permute-start | bytes 786440 | tf_op jit(solution)/shard_map/ppermute | solution.py:392
  89.6 3.6 %collective-permute-done.18.got = f32[512,128]{1,0:T(8,128)S(1)} collective-permute-done((f32[512,128]{1,0:T(8,128)S(1)}, f32[512,128]{1,0:T(8,128)S(1)}, u32[]{:S(2)}, u32[]{:S(2)}) %collective-permute-start.18) | collective-permute-done | bytes 262176 | tf_op jit(solution)/shard_map/ppermute | solution.py:392
  (56 shorter events, 9.0 us)
Async XLA Ops:
  2.1 5.9 %collective-permute-start = (f32[16,128]{1,0:T(8,128)}, f32[16,128]{1,0:T(8,128)S(1)}, u32[]{:S(2)}, u32[]{:S(2)}) collective-permute-start(f32[16,128]{1,0:T(8,128)} %pack.1.refs_0_.refs_1_), channel_id=1, source_target_pairs={{0,1},{1,0},{2,3},{3,2},{4,5},{5,4},{6,7},{7,6},{8,9},{9,8},{10,11... | collective-permute-start | bytes 24584 | tf_op jit(solution)/shard_map/ppermute | solution.py:443
  2.1 6.0 %collective-permute-start.1 = (f32[32,128,128]{2,1,0:T(8,128)}, f32[32,128,128]{2,1,0:T(8,128)S(1)}, u32[]{:S(2)}, u32[]{:S(2)}) collective-permute-start(f32[32,128,128]{2,1,0:T(8,128)} %refs_2_.1), channel_id=1, source_target_pairs={{0,1},{1,0},{2,3},{3,2},{4,5},{5,4},{6,7},{7,6},{8,9},{9,8},{10,11... | collective-permute-start | bytes 6291464 | tf_op jit(solution)/shard_map/ppermute | solution.py:441
  2.6 5.5 %copy-start.1 = (f32[32,128,128]{2,1,0:T(8,128)S(1)}, f32[32,128,128]{2,1,0:T(8,128)}, u32[]{:S(2)}) copy-start(f32[32,128,128]{2,1,0:T(8,128)} %refs_2_.1) | copy-start | bytes 6291460
  7.9 13.0 %collective-permute-start.2 = (f32[4360,128]{1,0:T(8,128)S(1)}, f32[4360,128]{1,0:T(8,128)S(1)}, u32[]{:S(2)}, u32[]{:S(2)}) collective-permute-start(f32[4360,128]{1,0:T(8,128)S(1)} %match.1.refs_4_), channel_id=1, source_target_pairs={{0,1},{1,0},{2,3},{3,2},{4,5},{5,4},{6,7},{7,6},{8,9},{9,8},{10,11... | collective-permute-start | bytes 6696968 | tf_op jit(solution)/shard_map/ppermute | solution.py:446
  15.3 19.1 %collective-permute-start.6 = (f32[8,160,128]{2,1,0:T(8,128)S(1)}, f32[8,160,128]{2,1,0:T(8,128)S(1)}, u32[]{:S(2)}, u32[]{:S(2)}) collective-permute-start(f32[8,160,128]{2,1,0:T(8,128)S(1)} %get-tuple-element.36), channel_id=1, source_target_pairs={{8,16},{3,5},{10,18},{11,13},{12,20},{19,21},{14,22},{27,29},{16,8... | collective-permute-start | bytes 1966088 | tf_op jit(solution)/shard_map/ppermute | solution.py:389
  19.5 17.1 %collective-permute-start.5 = (f32[8,184,128]{2,1,0:T(8,128)S(1)}, f32[8,184,128]{2,1,0:T(8,128)S(1)}, u32[]{:S(2)}, u32[]{:S(2)}) collective-permute-start(f32[8,184,128]{2,1,0:T(8,128)S(1)} %get-tuple-element.34), channel_id=1, source_target_pairs={{0,8},{1,3},{2,10},{9,11},{4,12},{17,19},{6,14},{25,27},{8,0},{3,1... | collective-permute-start | bytes 2261000 | tf_op jit(solution)/shard_map/ppermute | solution.py:389
  19.5 12.0 %collective-permute-start.7 = (f32[2,16,48,128]{3,2,1,0:T(8,128)S(1)}, f32[2,16,48,128]{3,2,1,0:T(8,128)S(1)}, u32[]{:S(2)}, u32[]{:S(2)}) collective-permute-start(f32[2,16,48,128]{3,2,1,0:T(8,128)S(1)} %get-tuple-element.38), channel_id=1, source_target_pairs={{0,32},{2,34},{4,36},{6,38},{8,40},{10,42},{12,44},{14,46},{16,48}... | collective-permute-start | bytes 2359304 | tf_op jit(solution)/shard_map/ppermute | solution.py:392
  26.5 16.2 %collective-permute-start.3 = (f32[8,256,128]{2,1,0:T(8,128)S(1)}, f32[8,256,128]{2,1,0:T(8,128)S(1)}, u32[]{:S(2)}, u32[]{:S(2)}) collective-permute-start(f32[8,256,128]{2,1,0:T(8,128)S(1)} %get-tuple-element.31), channel_id=1, source_target_pairs={{0,8},{1,3},{2,10},{9,11},{4,12},{17,19},{6,14},{25,27},{8,0},{3,1... | collective-permute-start | bytes 3145736 | tf_op jit(solution)/shard_map/ppermute | solution.py:389
  28.6 16.0 %collective-permute-start.4 = (f32[8,256,128]{2,1,0:T(8,128)S(1)}, f32[8,256,128]{2,1,0:T(8,128)S(1)}, u32[]{:S(2)}, u32[]{:S(2)}) collective-permute-start(f32[8,256,128]{2,1,0:T(8,128)S(1)} %get-tuple-element.32), channel_id=1, source_target_pairs={{8,16},{3,5},{10,18},{11,13},{12,20},{19,21},{14,22},{27,29},{16,8... | collective-permute-start | bytes 3145736 | tf_op jit(solution)/shard_map/ppermute | solution.py:389
  31.6 9.1 %collective-permute-start.10 = (f32[16,48,128]{2,1,0:T(8,128)S(1)}, f32[16,48,128]{2,1,0:T(8,128)S(1)}, u32[]{:S(2)}, u32[]{:S(2)}) collective-permute-start(f32[16,48,128]{2,1,0:T(8,128)S(1)} %get-tuple-element.55), channel_id=1, source_target_pairs={{32,64},{34,66},{36,68},{38,70},{40,72},{42,74},{44,76},{46,78},{4... | collective-permute-start | bytes 1179656 | tf_op jit(solution)/shard_map/ppermute | solution.py:392
  34.5 14.1 %collective-permute-start.14 = (f32[4,160,128]{2,1,0:T(8,128)S(1)}, f32[4,160,128]{2,1,0:T(8,128)S(1)}, u32[]{:S(2)}, u32[]{:S(2)}) collective-permute-start(f32[4,160,128]{2,1,0:T(8,128)S(1)} %get-tuple-element.59), channel_id=1, source_target_pairs={{0,8},{1,3},{2,10},{9,11},{4,12},{17,19},{6,14},{25,27},{8,0},{3,1... | collective-permute-start | bytes 983048 | tf_op jit(solution)/shard_map/ppermute | solution.py:389
  36.7 12.0 %collective-permute-start.13 = (f32[4,184,128]{2,1,0:T(8,128)S(1)}, f32[4,184,128]{2,1,0:T(8,128)S(1)}, u32[]{:S(2)}, u32[]{:S(2)}) collective-permute-start(f32[4,184,128]{2,1,0:T(8,128)S(1)} %get-tuple-element.57), channel_id=1, source_target_pairs={{8,16},{3,5},{10,18},{11,13},{12,20},{19,21},{14,22},{27,29},{16,8... | collective-permute-start | bytes 1130504 | tf_op jit(solution)/shard_map/ppermute | solution.py:389
  40.7 7.3 %collective-permute-start.11 = (f32[8,48,128]{2,1,0:T(8,128)S(1)}, f32[8,48,128]{2,1,0:T(8,128)S(1)}, u32[]{:S(2)}, u32[]{:S(2)}) collective-permute-start(f32[8,48,128]{2,1,0:T(8,128)S(1)} %get-tuple-element.65), channel_id=1, source_target_pairs={{0,8},{1,3},{2,10},{9,11},{4,12},{17,19},{6,14},{25,27},{8,0},{3,1... | collective-permute-start | bytes 589832 | tf_op jit(solution)/shard_map/ppermute | solution.py:389
  44.7 9.3 %collective-permute-start.9 = (f32[4,256,128]{2,1,0:T(8,128)S(1)}, f32[4,256,128]{2,1,0:T(8,128)S(1)}, u32[]{:S(2)}, u32[]{:S(2)}) collective-permute-start(f32[4,256,128]{2,1,0:T(8,128)S(1)} %get-tuple-element.52), channel_id=1, source_target_pairs={{0,8},{1,3},{2,10},{9,11},{4,12},{17,19},{6,14},{25,27},{8,0},{3,1... | collective-permute-start | bytes 1572872 | tf_op jit(solution)/shard_map/ppermute | solution.py:389
  45.0 10.5 %collective-permute-start.8 = (f32[4,256,128]{2,1,0:T(8,128)S(1)}, f32[4,256,128]{2,1,0:T(8,128)S(1)}, u32[]{:S(2)}, u32[]{:S(2)}) collective-permute-start(f32[4,256,128]{2,1,0:T(8,128)S(1)} %get-tuple-element.51), channel_id=1, source_target_pairs={{8,16},{3,5},{10,18},{11,13},{12,20},{19,21},{14,22},{27,29},{16,8... | collective-permute-start | bytes 1572872 | tf_op jit(solution)/shard_map/ppermute | solution.py:389
  48.0 11.9 %collective-permute-start.15 = (f32[4,48,128]{2,1,0:T(8,128)S(1)}, f32[4,48,128]{2,1,0:T(8,128)S(1)}, u32[]{:S(2)}, u32[]{:S(2)}) collective-permute-start(f32[4,48,128]{2,1,0:T(8,128)S(1)} %slice_add_fusion.24), channel_id=1, source_target_pairs={{8,16},{3,5},{10,18},{11,13},{12,20},{19,21},{14,22},{27,29},{16,8... | collective-permute-start | bytes 294920 | tf_op jit(solution)/shard_map/ppermute | solution.py:389
  55.6 11.4 %collective-permute-start.12 = (f32[2,512,128]{2,1,0:T(8,128)S(1)}, f32[2,512,128]{2,1,0:T(8,128)S(1)}, u32[]{:S(2)}, u32[]{:S(2)}) collective-permute-start(f32[2,512,128]{2,1,0:T(8,128)S(1)} %pad_maximum_fusion), channel_id=1, source_target_pairs={{2,4},{9,17},{10,12},{11,19},{18,20},{13,21},{26,28},{15,23},{4,2}... | collective-permute-start | bytes 1572872 | tf_op jit(solution)/shard_map/ppermute | solution.py:389
  59.9 7.9 %collective-permute-start.19 = (f32[2,392,128]{2,1,0:T(8,128)S(1)}, f32[2,392,128]{2,1,0:T(8,128)S(1)}, u32[]{:S(2)}, u32[]{:S(2)}) collective-permute-start(f32[2,392,128]{2,1,0:T(8,128)S(1)} %pad_maximum_fusion.1), channel_id=1, source_target_pairs={{0,2},{1,9},{8,10},{3,11},{16,18},{5,13},{24,26},{7,15},{2,0},{9,1... | collective-permute-start | bytes 1204232 | tf_op jit(solution)/shard_map/ppermute | solution.py:389
  67.9 7.0 %collective-permute-start.20 = (f32[1,392,128]{2,1,0:T(8,128)S(1)}, f32[1,392,128]{2,1,0:T(8,128)S(1)}, u32[]{:S(2)}, u32[]{:S(2)}) collective-permute-start(f32[1,392,128]{2,1,0:T(8,128)S(1)} %slice_add_fusion.14), channel_id=1, source_target_pairs={{2,4},{9,17},{10,12},{11,19},{18,20},{13,21},{26,28},{15,23},{4,2}... | collective-permute-start | bytes 602120 | tf_op jit(solution)/shard_map/ppermute | solution.py:389
  70.4 6.7 %collective-permute-start.16 = (f32[1,512,128]{2,1,0:T(8,128)S(1)}, f32[1,512,128]{2,1,0:T(8,128)S(1)}, u32[]{:S(2)}, u32[]{:S(2)}) collective-permute-start(f32[1,512,128]{2,1,0:T(8,128)S(1)} %fusion.5), channel_id=1, source_target_pairs={{0,2},{1,9},{8,10},{3,11},{16,18},{5,13},{24,26},{7,15},{2,0},{9,1... | collective-permute-start | bytes 786440 | tf_op jit(solution)/shard_map/ppermute | solution.py:389
  75.0 7.3 %collective-permute-start.21 = (f32[392,128]{1,0:T(8,128)S(1)}, f32[392,128]{1,0:T(8,128)S(1)}, u32[]{:S(2)}, u32[]{:S(2)}) collective-permute-start(f32[392,128]{1,0:T(8,128)S(1)} %bitcast.24), channel_id=1, source_target_pairs={{32,64},{34,66},{36,68},{38,70},{40,72},{42,74},{44,76},{46,78},{4... | collective-permute-start | bytes 602120 | tf_op jit(solution)/shard_map/ppermute | solution.py:392
  77.2 8.3 %collective-permute-start.17 = (f32[512,128]{1,0:T(8,128)S(1)}, f32[512,128]{1,0:T(8,128)S(1)}, u32[]{:S(2)}, u32[]{:S(2)}) collective-permute-start(f32[512,128]{1,0:T(8,128)S(1)} %fusion.4), channel_id=1, source_target_pairs={{0,32},{2,34},{4,36},{6,38},{8,40},{10,42},{12,44},{14,46},{16,48}... | collective-permute-start | bytes 786440 | tf_op jit(solution)/shard_map/ppermute | solution.py:392
  82.3 6.1 %collective-permute-start.22 = (f32[440,128]{1,0:T(8,128)S(1)}, f32[440,128]{1,0:T(8,128)S(1)}, u32[]{:S(2)}, u32[]{:S(2)}) collective-permute-start(f32[440,128]{1,0:T(8,128)S(1)} %pad_maximum_fusion.4.var), channel_id=1, source_target_pairs={{0,32},{2,34},{4,36},{6,38},{8,40},{10,42},{12,44},{14,46},{16,48}... | collective-permute-start | bytes 675848 | tf_op jit(solution)/shard_map/ppermute | solution.py:392
  85.5 7.7 %collective-permute-start.18 = (f32[512,128]{1,0:T(8,128)S(1)}, f32[512,128]{1,0:T(8,128)S(1)}, u32[]{:S(2)}, u32[]{:S(2)}) collective-permute-start(f32[512,128]{1,0:T(8,128)S(1)} %add.129.num), channel_id=1, source_target_pairs={{32,64},{34,66},{36,68},{38,70},{40,72},{42,74},{44,76},{46,78},{4... | collective-permute-start | bytes 786440 | tf_op jit(solution)/shard_map/ppermute | solution.py:392
  (1 other events, 5.5 us)

commit v2 on v1

--- a/solution.py
+++ b/solution.py
@@ -428,7 +428,8 @@
     (v_got,) = after((v_got,), n_send)
     v, v_send = fold(v, v_got)
     n = n[0] + cross(n_send, 1, 0)[0]
-    v = v[0] + cross(v_send, 1, 1)[0]
+    (v_got,) = after((cross(v_send, 1, 1),), n)
+    v = v[0] + v_got[0]
 
     n = n + visit(n, 0)
     v_got, main = visit(v, 1), 2 * MAIN + META

time: 94.1 us -> 90.9 us (0.966); the launches traced: 93.9 us -> 92.1 us
  starting transfers between devices: 28.9 us -> 27.7 us
    ppermute x6, starting transfers between devices: 9.81 us -> 8.27 us  [visit(): return lax.ppermute(x, ('visit', 'patch'), over_visit(edge))]
where the time goes in v2:
time: 90.9 us; the launch traced here: 92.1 us
  waiting for transfers between devices  41 us (45%)
  starting transfers between devices  27.7 us (30%)
  Pallas kernels  21.5 us (24%)
  other arithmetic  1.1 us (1%)
    ppermute x14, waiting for transfers between devices, cross(): return lax.ppermute(x, 'patch', over_patch(axis, edge))  23.3 us
    ppermute x14, starting transfers between devices, cross(): return lax.ppermute(x, 'patch', over_patch(axis, edge))  18.8 us
    ppermute x6, waiting for transfers between devices, visit(): return lax.ppermute(x, ('visit', 'patch'), over_visit(edge))  17.6 us
    pallas_call x2, Pallas kernels, warp(): pl.pallas_call(functools.partial(warp_kernel, with_meta), out_shape=outs,...  12.7 us
    ppermute x6, starting transfers between devices, visit(): return lax.ppermute(x, ('visit', 'patch'), over_visit(edge))  8.27 us
    pallas_call x1, Pallas kernels, match(): pl.pallas_call(match_kernel, out_shape=jax.ShapeDtypeStruct((TILES * PITC...  5.34 us
    pallas_call x2, Pallas kernels, finish(): pl.pallas_call(kernel, out_shape=[jax.ShapeDtypeStruct((PATCH, PATCH), F3...  2.01 us
  transfers between devices with their start and end apart: 23, of which 14 were waited for; matrix products, arithmetic and copies ran while one was open for 1% of the time, Pallas kernels for 21%

profile of v2, /device:TPU:0, one launch (start us, length us, event | category | flops | bytes accessed | tf_op | source)
XLA Modules:
  0.0 92.1 jit_solution(10830562603180336182)
XLA Ops:
  0.6 1.4 %pack.1.refs_0_.refs_1_ = f32[16,128]{1,0:T(8,128)} custom-call(s32[2,32]{1,0:T(2,128)} %bitcast.27, s32[2,2,32]{2,1,0:T(2,128)} %bitcast.25, f32[2,2,32]{2,1,0:T(2,128)} %bitcast.26), custom_call_target="tpu_custom_call" | custom-call | tf_op jit(solution)/shard_map/pack/pallas_call | solution.py:89
  2.6 5.3 %match.1.refs_4_ = f32[4360,128]{1,0:T(8,128)S(1)} custom-call(s32[3,32]{1,0:T(4,128)} %bitcast.28, f32[3,32]{1,0:T(4,128)} %bitcast.29, f32[8,2,41]{2,1,0:T(2,128)} %taps_hbm.1, f32[32,128,128]{2,1,0:T(8,128)} %image_hbm.1), custom_call_target="tpu_custom_call" | custom-call | flops 99999997952 | bytes 6291456 | tf_op jit(solution)/shard_map/match/pallas_call | solution.py:157
  8.1 7.2 %warp_meta.1 = (f32[8,184,128]{2,1,0:T(8,128)S(1)}, f32[8,184,128]{2,1,0:T(8,128)S(1)}, f32[8,160,128]{2,1,0:T(8,128)S(1)}, f32[8,160,128]{2,1,0:T(8,128)S(1)}, ...) custom-call(f32[16,128]{1,0:T(8,128)S(1)} %copy-done, ...), custom_call_target="tpu_custom_call" | custom-call | flops 10000000000 | bytes 8388608 | tf_op jit(solution)/shard_map/warp_meta/pallas_call | solution.py:298
  15.3 4.2 %collective-permute-start.6 = (f32[8,160,128]{2,1,0:T(8,128)S(1)}, f32[8,160,128]{2,1,0:T(8,128)S(1)}, u32[]{:S(2)}, u32[]{:S(2)}) collective-permute-start(f32[8,160,128]{2,1,0:T(8,128)S(1)} %get-tuple-element.37), channel_id=1, source_target_pairs={{8,16},{3,5},{10,18},{11,13},{12,20},{19,21},{14,22},{27,29},{16,8... | collective-permute-start | bytes 1966088 | tf_op jit(solution)/shard_map/ppermute | solution.py:389
  19.5 1.5 %collective-permute-start.7 = (f32[2,16,48,128]{3,2,1,0:T(8,128)S(1)}, f32[2,16,48,128]{3,2,1,0:T(8,128)S(1)}, u32[]{:S(2)}, u32[]{:S(2)}) collective-permute-start(f32[2,16,48,128]{3,2,1,0:T(8,128)S(1)} %get-tuple-element.39), channel_id=1, source_target_pairs={{0,32},{2,34},{4,36},{6,38},{8,40},{10,42},{12,44},{14,46},{16,48}... | collective-permute-start | bytes 2359304 | tf_op jit(solution)/shard_map/ppermute | solution.py:392
  21.0 5.5 %warp.1 = (f32[8,256,128]{2,1,0:T(8,128)S(1)}, f32[8,256,128]{2,1,0:T(8,128)S(1)}, f32[8,256,128]{2,1,0:T(8,128)S(1)}, f32[8,256,128]{2,1,0:T(8,128)S(1)}) custom-call(s32[2,128]{1,0:T(2,128)S(1)} %get-tuple-element.28.refs_0_, f32[16,128]{1,0:T(8,128)S(1)} %copy-done, f32[16,128]{1,0:T(8,128)S(1)} %collective-permute-done.refs_1_.refs_2_, ...), custom_call_target="tpu_custom_call" | custom-call | flops 10000000000 | bytes 8388608 | tf_op jit(solution)/shard_map/warp/pallas_call | solution.py:298
  26.5 2.1 %collective-permute-start.3 = (f32[8,256,128]{2,1,0:T(8,128)S(1)}, f32[8,256,128]{2,1,0:T(8,128)S(1)}, u32[]{:S(2)}, u32[]{:S(2)}) collective-permute-start(f32[8,256,128]{2,1,0:T(8,128)S(1)} %get-tuple-element.32), channel_id=1, source_target_pairs={{0,8},{1,3},{2,10},{9,11},{4,12},{17,19},{6,14},{25,27},{8,0},{3,1... | collective-permute-start | bytes 3145736 | tf_op jit(solution)/shard_map/ppermute | solution.py:389
  28.7 2.8 %collective-permute-done.7 = f32[2,16,48,128]{3,2,1,0:T(8,128)S(1)} collective-permute-done((f32[2,16,48,128]{3,2,1,0:T(8,128)S(1)}, f32[2,16,48,128]{3,2,1,0:T(8,128)S(1)}, u32[]{:S(2)}, u32[]{:S(2)}) %collective-permute-start.7) | collective-permute-done | bytes 786464 | tf_op jit(solution)/shard_map/ppermute | solution.py:392
  31.6 2.8 %collective-permute-start.10 = (f32[16,48,128]{2,1,0:T(8,128)S(1)}, f32[16,48,128]{2,1,0:T(8,128)S(1)}, u32[]{:S(2)}, u32[]{:S(2)}) collective-permute-start(f32[16,48,128]{2,1,0:T(8,128)S(1)} %get-tuple-element.57), channel_id=1, source_target_pairs={{32,64},{34,66},{36,68},{38,70},{40,72},{42,74},{44,76},{46,78},{4... | collective-permute-start | bytes 1179656 | tf_op jit(solution)/shard_map/ppermute | solution.py:392
  34.5 2.1 %collective-permute-start.14 = (f32[4,160,128]{2,1,0:T(8,128)S(1)}, f32[4,160,128]{2,1,0:T(8,128)S(1)}, u32[]{:S(2)}, u32[]{:S(2)}) collective-permute-start(f32[4,160,128]{2,1,0:T(8,128)S(1)} %get-tuple-element.61), channel_id=1, source_target_pairs={{0,8},{1,3},{2,10},{9,11},{4,12},{17,19},{6,14},{25,27},{8,0},{3,1... | collective-permute-start | bytes 983048 | tf_op jit(solution)/shard_map/ppermute | solution.py:389
  36.9 3.8 %collective-permute-done.10 = f32[16,48,128]{2,1,0:T(8,128)S(1)} collective-permute-done((f32[16,48,128]{2,1,0:T(8,128)S(1)}, f32[16,48,128]{2,1,0:T(8,128)S(1)}, u32[]{:S(2)}, u32[]{:S(2)}) %collective-permute-start.10) | collective-permute-done | bytes 393248 | tf_op jit(solution)/shard_map/ppermute | solution.py:392
  40.7 2.1 %collective-permute-start.11 = (f32[8,48,128]{2,1,0:T(8,128)S(1)}, f32[8,48,128]{2,1,0:T(8,128)S(1)}, u32[]{:S(2)}, u32[]{:S(2)}) collective-permute-start(f32[8,48,128]{2,1,0:T(8,128)S(1)} %get-tuple-element.67), channel_id=1, source_target_pairs={{0,8},{1,3},{2,10},{9,11},{4,12},{17,19},{6,14},{25,27},{8,0},{3,1... | collective-permute-start | bytes 589832 | tf_op jit(solution)/shard_map/ppermute | solution.py:389
  42.8 1.8 %collective-permute-done.4 = f32[8,256,128]{2,1,0:T(8,128)S(1)} collective-permute-done((f32[8,256,128]{2,1,0:T(8,128)S(1)}, f32[8,256,128]{2,1,0:T(8,128)S(1)}, u32[]{:S(2)}, u32[]{:S(2)}) %collective-permute-start.4) | collective-permute-done | bytes 1048608 | tf_op jit(solution)/shard_map/ppermute | solution.py:389
  45.1 2.9 %collective-permute-done.11 = f32[8,48,128]{2,1,0:T(8,128)S(1)} collective-permute-done((f32[8,48,128]{2,1,0:T(8,128)S(1)}, f32[8,48,128]{2,1,0:T(8,128)S(1)}, u32[]{:S(2)}, u32[]{:S(2)}) %collective-permute-start.11) | collective-permute-done | bytes 196640 | tf_op jit(solution)/shard_map/ppermute | solution.py:389
  48.8 5.2 %collective-permute-done.9 = f32[4,256,128]{2,1,0:T(8,128)S(1)} collective-permute-done((f32[4,256,128]{2,1,0:T(8,128)S(1)}, f32[4,256,128]{2,1,0:T(8,128)S(1)}, u32[]{:S(2)}, u32[]{:S(2)}) %collective-permute-start.9) | collective-permute-done | bytes 524320 | tf_op jit(solution)/shard_map/ppermute | solution.py:389
  54.0 1.4 %collective-permute-done.8 = f32[4,256,128]{2,1,0:T(8,128)S(1)} collective-permute-done((f32[4,256,128]{2,1,0:T(8,128)S(1)}, f32[4,256,128]{2,1,0:T(8,128)S(1)}, u32[]{:S(2)}, u32[]{:S(2)}) %collective-permute-start.8) | collective-permute-done | bytes 524320 | tf_op jit(solution)/shard_map/ppermute | solution.py:389
  55.6 4.4 %collective-permute-start.12 = (f32[2,512,128]{2,1,0:T(8,128)S(1)}, f32[2,512,128]{2,1,0:T(8,128)S(1)}, u32[]{:S(2)}, u32[]{:S(2)}) collective-permute-start(f32[2,512,128]{2,1,0:T(8,128)S(1)} %pad_maximum_fusion), channel_id=1, source_target_pairs={{2,4},{9,17},{10,12},{11,19},{18,20},{13,21},{26,28},{15,23},{4,2}... | collective-permute-start | bytes 1572872 | tf_op jit(solution)/shard_map/ppermute | solution.py:389
  60.1 7.0 %collective-permute-done.12 = f32[2,512,128]{2,1,0:T(8,128)S(1)} collective-permute-done((f32[2,512,128]{2,1,0:T(8,128)S(1)}, f32[2,512,128]{2,1,0:T(8,128)S(1)}, u32[]{:S(2)}, u32[]{:S(2)}) %collective-permute-start.12) | collective-permute-done | bytes 524320 | tf_op jit(solution)/shard_map/ppermute | solution.py:389
  68.0 2.6 %collective-permute-start.20 = (f32[1,392,128]{2,1,0:T(8,128)S(1)}, f32[1,392,128]{2,1,0:T(8,128)S(1)}, u32[]{:S(2)}, u32[]{:S(2)}) collective-permute-start(f32[1,392,128]{2,1,0:T(8,128)S(1)} %slice_add_fusion.14), channel_id=1, source_target_pairs={{2,4},{9,17},{10,12},{11,19},{18,20},{13,21},{26,28},{15,23},{4,2}... | collective-permute-start | bytes 602120 | tf_op jit(solution)/shard_map/ppermute | solution.py:389
  70.6 3.0 %collective-permute-done.16 = f32[1,512,128]{2,1,0:T(8,128)S(1)} collective-permute-done((f32[1,512,128]{2,1,0:T(8,128)S(1)}, f32[1,512,128]{2,1,0:T(8,128)S(1)}, u32[]{:S(2)}, u32[]{:S(2)}) %collective-permute-start.16) | collective-permute-done | bytes 262176 | tf_op jit(solution)/shard_map/ppermute | solution.py:389
  75.0 2.4 %collective-permute-start.21 = (f32[392,128]{1,0:T(8,128)S(1)}, f32[392,128]{1,0:T(8,128)S(1)}, u32[]{:S(2)}, u32[]{:S(2)}) collective-permute-start(f32[392,128]{1,0:T(8,128)S(1)} %bitcast.24), channel_id=1, source_target_pairs={{32,64},{34,66},{36,68},{38,70},{40,72},{42,74},{44,76},{46,78},{4... | collective-permute-start | bytes 602120 | tf_op jit(solution)/shard_map/ppermute | solution.py:392
  77.5 6.0 %collective-permute-done.21 = f32[392,128]{1,0:T(8,128)S(1)} collective-permute-done((f32[392,128]{1,0:T(8,128)S(1)}, f32[392,128]{1,0:T(8,128)S(1)}, u32[]{:S(2)}, u32[]{:S(2)}) %collective-permute-start.21) | collective-permute-done | bytes 200736 | tf_op jit(solution)/shard_map/ppermute | solution.py:392
  83.7 1.3 %collective-permute-start.18 = (f32[512,128]{1,0:T(8,128)S(1)}, f32[512,128]{1,0:T(8,128)S(1)}, u32[]{:S(2)}, u32[]{:S(2)}) collective-permute-start(f32[512,128]{1,0:T(8,128)S(1)} %add.129.num), channel_id=1, source_target_pairs={{32,64},{34,66},{36,68},{38,70},{40,72},{42,74},{44,76},{46,78},{4... | collective-permute-start | bytes 786440 | tf_op jit(solution)/shard_map/ppermute | solution.py:392
  85.0 4.6 %collective-permute-done.22.got = f32[440,128]{1,0:T(8,128)S(1)} collective-permute-done((f32[440,128]{1,0:T(8,128)S(1)}, f32[440,128]{1,0:T(8,128)S(1)}, u32[]{:S(2)}, u32[]{:S(2)}) %collective-permute-start.22) | collective-permute-done | bytes 225312 | tf_op jit(solution)/shard_map/ppermute | solution.py:392
  (56 shorter events, 7.7 us)
Async XLA Ops:
  2.1 5.9 %collective-permute-start = (f32[16,128]{1,0:T(8,128)}, f32[16,128]{1,0:T(8,128)S(1)}, u32[]{:S(2)}, u32[]{:S(2)}) collective-permute-start(f32[16,128]{1,0:T(8,128)} %pack.1.refs_0_.refs_1_), channel_id=1, source_target_pairs={{0,1},{1,0},{2,3},{3,2},{4,5},{5,4},{6,7},{7,6},{8,9},{9,8},{10,11... | collective-permute-start | bytes 24584 | tf_op jit(solution)/shard_map/ppermute | solution.py:444
  2.1 6.0 %collective-permute-start.1 = (f32[32,128,128]{2,1,0:T(8,128)}, f32[32,128,128]{2,1,0:T(8,128)S(1)}, u32[]{:S(2)}, u32[]{:S(2)}) collective-permute-start(f32[32,128,128]{2,1,0:T(8,128)} %refs_2_.1), channel_id=1, source_target_pairs={{0,1},{1,0},{2,3},{3,2},{4,5},{5,4},{6,7},{7,6},{8,9},{9,8},{10,11... | collective-permute-start | bytes 6291464 | tf_op jit(solution)/shard_map/ppermute | solution.py:442
  2.6 5.5 %copy-start.1 = (f32[32,128,128]{2,1,0:T(8,128)S(1)}, f32[32,128,128]{2,1,0:T(8,128)}, u32[]{:S(2)}) copy-start(f32[32,128,128]{2,1,0:T(8,128)} %refs_2_.1) | copy-start | bytes 6291460
  7.9 13.0 %collective-permute-start.2 = (f32[4360,128]{1,0:T(8,128)S(1)}, f32[4360,128]{1,0:T(8,128)S(1)}, u32[]{:S(2)}, u32[]{:S(2)}) collective-permute-start(f32[4360,128]{1,0:T(8,128)S(1)} %match.1.refs_4_), channel_id=1, source_target_pairs={{0,1},{1,0},{2,3},{3,2},{4,5},{5,4},{6,7},{7,6},{8,9},{9,8},{10,11... | collective-permute-start | bytes 6696968 | tf_op jit(solution)/shard_map/ppermute | solution.py:447
  15.3 19.1 %collective-permute-start.6 = (f32[8,160,128]{2,1,0:T(8,128)S(1)}, f32[8,160,128]{2,1,0:T(8,128)S(1)}, u32[]{:S(2)}, u32[]{:S(2)}) collective-permute-start(f32[8,160,128]{2,1,0:T(8,128)S(1)} %get-tuple-element.37), channel_id=1, source_target_pairs={{8,16},{3,5},{10,18},{11,13},{12,20},{19,21},{14,22},{27,29},{16,8... | collective-permute-start | bytes 1966088 | tf_op jit(solution)/shard_map/ppermute | solution.py:389
  19.5 17.1 %collective-permute-start.5 = (f32[8,184,128]{2,1,0:T(8,128)S(1)}, f32[8,184,128]{2,1,0:T(8,128)S(1)}, u32[]{:S(2)}, u32[]{:S(2)}) collective-permute-start(f32[8,184,128]{2,1,0:T(8,128)S(1)} %get-tuple-element.35), channel_id=1, source_target_pairs={{0,8},{1,3},{2,10},{9,11},{4,12},{17,19},{6,14},{25,27},{8,0},{3,1... | collective-permute-start | bytes 2261000 | tf_op jit(solution)/shard_map/ppermute | solution.py:389
  19.5 12.0 %collective-permute-start.7 = (f32[2,16,48,128]{3,2,1,0:T(8,128)S(1)}, f32[2,16,48,128]{3,2,1,0:T(8,128)S(1)}, u32[]{:S(2)}, u32[]{:S(2)}) collective-permute-start(f32[2,16,48,128]{3,2,1,0:T(8,128)S(1)} %get-tuple-element.39), channel_id=1, source_target_pairs={{0,32},{2,34},{4,36},{6,38},{8,40},{10,42},{12,44},{14,46},{16,48}... | collective-permute-start | bytes 2359304 | tf_op jit(solution)/shard_map/ppermute | solution.py:392
  26.5 16.3 %collective-permute-start.3 = (f32[8,256,128]{2,1,0:T(8,128)S(1)}, f32[8,256,128]{2,1,0:T(8,128)S(1)}, u32[]{:S(2)}, u32[]{:S(2)}) collective-permute-start(f32[8,256,128]{2,1,0:T(8,128)S(1)} %get-tuple-element.32), channel_id=1, source_target_pairs={{0,8},{1,3},{2,10},{9,11},{4,12},{17,19},{6,14},{25,27},{8,0},{3,1... | collective-permute-start | bytes 3145736 | tf_op jit(solution)/shard_map/ppermute | solution.py:389
  28.6 16.0 %collective-permute-start.4 = (f32[8,256,128]{2,1,0:T(8,128)S(1)}, f32[8,256,128]{2,1,0:T(8,128)S(1)}, u32[]{:S(2)}, u32[]{:S(2)}) collective-permute-start(f32[8,256,128]{2,1,0:T(8,128)S(1)} %get-tuple-element.33), channel_id=1, source_target_pairs={{8,16},{3,5},{10,18},{11,13},{12,20},{19,21},{14,22},{27,29},{16,8... | collective-permute-start | bytes 3145736 | tf_op jit(solution)/shard_map/ppermute | solution.py:389
  31.6 9.1 %collective-permute-start.10 = (f32[16,48,128]{2,1,0:T(8,128)S(1)}, f32[16,48,128]{2,1,0:T(8,128)S(1)}, u32[]{:S(2)}, u32[]{:S(2)}) collective-permute-start(f32[16,48,128]{2,1,0:T(8,128)S(1)} %get-tuple-element.57), channel_id=1, source_target_pairs={{32,64},{34,66},{36,68},{38,70},{40,72},{42,74},{44,76},{46,78},{4... | collective-permute-start | bytes 1179656 | tf_op jit(solution)/shard_map/ppermute | solution.py:392
  34.5 14.1 %collective-permute-start.14 = (f32[4,160,128]{2,1,0:T(8,128)S(1)}, f32[4,160,128]{2,1,0:T(8,128)S(1)}, u32[]{:S(2)}, u32[]{:S(2)}) collective-permute-start(f32[4,160,128]{2,1,0:T(8,128)S(1)} %get-tuple-element.61), channel_id=1, source_target_pairs={{0,8},{1,3},{2,10},{9,11},{4,12},{17,19},{6,14},{25,27},{8,0},{3,1... | collective-permute-start | bytes 983048 | tf_op jit(solution)/shard_map/ppermute | solution.py:389
  36.7 12.0 %collective-permute-start.13 = (f32[4,184,128]{2,1,0:T(8,128)S(1)}, f32[4,184,128]{2,1,0:T(8,128)S(1)}, u32[]{:S(2)}, u32[]{:S(2)}) collective-permute-start(f32[4,184,128]{2,1,0:T(8,128)S(1)} %get-tuple-element.59), channel_id=1, source_target_pairs={{8,16},{3,5},{10,18},{11,13},{12,20},{19,21},{14,22},{27,29},{16,8... | collective-permute-start | bytes 1130504 | tf_op jit(solution)/shard_map/ppermute | solution.py:389
  40.7 7.3 %collective-permute-start.11 = (f32[8,48,128]{2,1,0:T(8,128)S(1)}, f32[8,48,128]{2,1,0:T(8,128)S(1)}, u32[]{:S(2)}, u32[]{:S(2)}) collective-permute-start(f32[8,48,128]{2,1,0:T(8,128)S(1)} %get-tuple-element.67), channel_id=1, source_target_pairs={{0,8},{1,3},{2,10},{9,11},{4,12},{17,19},{6,14},{25,27},{8,0},{3,1... | collective-permute-start | bytes 589832 | tf_op jit(solution)/shard_map/ppermute | solution.py:389
  44.7 9.3 %collective-permute-start.9 = (f32[4,256,128]{2,1,0:T(8,128)S(1)}, f32[4,256,128]{2,1,0:T(8,128)S(1)}, u32[]{:S(2)}, u32[]{:S(2)}) collective-permute-start(f32[4,256,128]{2,1,0:T(8,128)S(1)} %get-tuple-element.54), channel_id=1, source_target_pairs={{0,8},{1,3},{2,10},{9,11},{4,12},{17,19},{6,14},{25,27},{8,0},{3,1... | collective-permute-start | bytes 1572872 | tf_op jit(solution)/shard_map/ppermute | solution.py:389
  45.0 10.5 %collective-permute-start.8 = (f32[4,256,128]{2,1,0:T(8,128)S(1)}, f32[4,256,128]{2,1,0:T(8,128)S(1)}, u32[]{:S(2)}, u32[]{:S(2)}) collective-permute-start(f32[4,256,128]{2,1,0:T(8,128)S(1)} %get-tuple-element.53), channel_id=1, source_target_pairs={{8,16},{3,5},{10,18},{11,13},{12,20},{19,21},{14,22},{27,29},{16,8... | collective-permute-start | bytes 1572872 | tf_op jit(solution)/shard_map/ppermute | solution.py:389
  48.0 12.0 %collective-permute-start.15 = (f32[4,48,128]{2,1,0:T(8,128)S(1)}, f32[4,48,128]{2,1,0:T(8,128)S(1)}, u32[]{:S(2)}, u32[]{:S(2)}) collective-permute-start(f32[4,48,128]{2,1,0:T(8,128)S(1)} %slice_add_fusion.24), channel_id=1, source_target_pairs={{8,16},{3,5},{10,18},{11,13},{12,20},{19,21},{14,22},{27,29},{16,8... | collective-permute-start | bytes 294920 | tf_op jit(solution)/shard_map/ppermute | solution.py:389
  55.6 11.5 %collective-permute-start.12 = (f32[2,512,128]{2,1,0:T(8,128)S(1)}, f32[2,512,128]{2,1,0:T(8,128)S(1)}, u32[]{:S(2)}, u32[]{:S(2)}) collective-permute-start(f32[2,512,128]{2,1,0:T(8,128)S(1)} %pad_maximum_fusion), channel_id=1, source_target_pairs={{2,4},{9,17},{10,12},{11,19},{18,20},{13,21},{26,28},{15,23},{4,2}... | collective-permute-start | bytes 1572872 | tf_op jit(solution)/shard_map/ppermute | solution.py:389
  60.0 7.9 %collective-permute-start.19 = (f32[2,392,128]{2,1,0:T(8,128)S(1)}, f32[2,392,128]{2,1,0:T(8,128)S(1)}, u32[]{:S(2)}, u32[]{:S(2)}) collective-permute-start(f32[2,392,128]{2,1,0:T(8,128)S(1)} %pad_maximum_fusion.1), channel_id=1, source_target_pairs={{0,2},{1,9},{8,10},{3,11},{16,18},{5,13},{24,26},{7,15},{2,0},{9,1... | collective-permute-start | bytes 1204232 | tf_op jit(solution)/shard_map/ppermute | solution.py:389
  67.2 6.5 %collective-permute-start.16 = (f32[1,512,128]{2,1,0:T(8,128)S(1)}, f32[1,512,128]{2,1,0:T(8,128)S(1)}, u32[]{:S(2)}, u32[]{:S(2)}) collective-permute-start(f32[1,512,128]{2,1,0:T(8,128)S(1)} %fusion.5), channel_id=1, source_target_pairs={{0,2},{1,9},{8,10},{3,11},{16,18},{5,13},{24,26},{7,15},{2,0},{9,1... | collective-permute-start | bytes 786440 | tf_op jit(solution)/shard_map/ppermute | solution.py:389
  68.0 7.0 %collective-permute-start.20 = (f32[1,392,128]{2,1,0:T(8,128)S(1)}, f32[1,392,128]{2,1,0:T(8,128)S(1)}, u32[]{:S(2)}, u32[]{:S(2)}) collective-permute-start(f32[1,392,128]{2,1,0:T(8,128)S(1)} %slice_add_fusion.14), channel_id=1, source_target_pairs={{2,4},{9,17},{10,12},{11,19},{18,20},{13,21},{26,28},{15,23},{4,2}... | collective-permute-start | bytes 602120 | tf_op jit(solution)/shard_map/ppermute | solution.py:389
  73.7 10.0 %collective-permute-start.17 = (f32[512,128]{1,0:T(8,128)S(1)}, f32[512,128]{1,0:T(8,128)S(1)}, u32[]{:S(2)}, u32[]{:S(2)}) collective-permute-start(f32[512,128]{1,0:T(8,128)S(1)} %fusion.4), channel_id=1, source_target_pairs={{0,32},{2,34},{4,36},{6,38},{8,40},{10,42},{12,44},{14,46},{16,48}... | collective-permute-start | bytes 786440 | tf_op jit(solution)/shard_map/ppermute | solution.py:392
  75.0 8.4 %collective-permute-start.21 = (f32[392,128]{1,0:T(8,128)S(1)}, f32[392,128]{1,0:T(8,128)S(1)}, u32[]{:S(2)}, u32[]{:S(2)}) collective-permute-start(f32[392,128]{1,0:T(8,128)S(1)} %bitcast.24), channel_id=1, source_target_pairs={{32,64},{34,66},{36,68},{38,70},{40,72},{42,74},{44,76},{46,78},{4... | collective-permute-start | bytes 602120 | tf_op jit(solution)/shard_map/ppermute | solution.py:392
  83.5 6.1 %collective-permute-start.22 = (f32[440,128]{1,0:T(8,128)S(1)}, f32[440,128]{1,0:T(8,128)S(1)}, u32[]{:S(2)}, u32[]{:S(2)}) collective-permute-start(f32[440,128]{1,0:T(8,128)S(1)} %pad_maximum_fusion.4.var), channel_id=1, source_target_pairs={{0,32},{2,34},{4,36},{6,38},{8,40},{10,42},{12,44},{14,46},{16,48}... | collective-permute-start | bytes 675848 | tf_op jit(solution)/shard_map/ppermute | solution.py:392
  83.7 7.7 %collective-permute-start.18 = (f32[512,128]{1,0:T(8,128)S(1)}, f32[512,128]{1,0:T(8,128)S(1)}, u32[]{:S(2)}, u32[]{:S(2)}) collective-permute-start(f32[512,128]{1,0:T(8,128)S(1)} %add.129.num), channel_id=1, source_target_pairs={{32,64},{34,66},{36,68},{38,70},{40,72},{42,74},{44,76},{46,78},{4... | collective-permute-start | bytes 786440 | tf_op jit(solution)/shard_map/ppermute | solution.py:392
  (1 other events, 5.5 us)

commit v3 on v2

--- a/solution.py
+++ b/solution.py
@@ -24,7 +24,7 @@
 BF16 = jnp.bfloat16
 
 EMPTY = 1 << 24
-UNROLL = 8
+UNROLL = 12
 MATCH_UNROLL = 16
 CHUNKS = 2
 MATCH_COST = 100_000_000_000

time: 90.9 us -> 90.2 us (level); the launches traced: 92.1 us -> 90.1 us
  waiting for transfers between devices: 41 us -> 39 us
  Pallas kernels: 21.5 us -> 20.4 us
  starting transfers between devices: 27.7 us -> 28.8 us
    ppermute x6, starting transfers between devices: 8.27 us -> 10.4 us  [visit(): return lax.ppermute(x, ('visit', 'patch'), over_visit(edge))]
    pallas_call x2, Pallas kernels: 12.7 us -> 11.6 us  [warp(): pl.pallas_call(functools.partial(warp_kernel, with_meta), out_shape=outs,...]
    ppermute x14, starting transfers between devices: 18.8 us -> 17.7 us  [cross(): return lax.ppermute(x, 'patch', over_patch(axis, edge))]
    ppermute x14, waiting for transfers between devices: 23.3 us -> 22.3 us  [cross(): return lax.ppermute(x, 'patch', over_patch(axis, edge))]
    ppermute x6, waiting for transfers between devices: 17.6 us -> 16.7 us  [visit(): return lax.ppermute(x, ('visit', 'patch'), over_visit(edge))]
  transfers between devices with their start and end apart: 23 -> 23, of which waited for: 14 -> 13; matrix products, arithmetic and copies ran while one was open for 1% -> 1% of each run, Pallas kernels for 21% -> 20%
where the time goes in v3:
time: 90.2 us; the launch traced here: 90.1 us
  waiting for transfers between devices  39 us (43%)
  starting transfers between devices  28.8 us (32%)
  Pallas kernels  20.4 us (23%)
  other arithmetic  1.1 us (1%)
    ppermute x14, waiting for transfers between devices, cross(): return lax.ppermute(x, 'patch', over_patch(axis, edge))  22.3 us
    ppermute x14, starting transfers between devices, cross(): return lax.ppermute(x, 'patch', over_patch(axis, edge))  17.7 us
    ppermute x6, waiting for transfers between devices, visit(): return lax.ppermute(x, ('visit', 'patch'), over_visit(edge))  16.7 us
    pallas_call x2, Pallas kernels, warp(): pl.pallas_call(functools.partial(warp_kernel, with_meta), out_shape=outs,...  11.6 us
    ppermute x6, starting transfers between devices, visit(): return lax.ppermute(x, ('visit', 'patch'), over_visit(edge))  10.4 us
    pallas_call x1, Pallas kernels, match(): pl.pallas_call(match_kernel, out_shape=jax.ShapeDtypeStruct((TILES * PITC...  5.34 us
    pallas_call x2, Pallas kernels, finish(): pl.pallas_call(kernel, out_shape=[jax.ShapeDtypeStruct((PATCH, PATCH), F3...  2.01 us
  transfers between devices with their start and end apart: 23, of which 13 were waited for; matrix products, arithmetic and copies ran while one was open for 1% of the time, Pallas kernels for 20%

profile of v3, /device:TPU:0, one launch (start us, length us, event | category | flops | bytes accessed | tf_op | source)
XLA Modules:
  0.0 90.1 jit_solution(16136979683079195311)
XLA Ops:
  0.6 1.4 %pack.1.refs_0_.refs_1_ = f32[16,128]{1,0:T(8,128)} custom-call(s32[2,32]{1,0:T(2,128)} %bitcast.27, s32[2,2,32]{2,1,0:T(2,128)} %bitcast.25, f32[2,2,32]{2,1,0:T(2,128)} %bitcast.26), custom_call_target="tpu_custom_call" | custom-call | tf_op jit(solution)/shard_map/pack/pallas_call | solution.py:89
  2.6 5.3 %match.1.refs_4_ = f32[4360,128]{1,0:T(8,128)S(1)} custom-call(s32[3,32]{1,0:T(4,128)} %bitcast.28, f32[3,32]{1,0:T(4,128)} %bitcast.29, f32[8,2,41]{2,1,0:T(2,128)} %taps_hbm.1, f32[32,128,128]{2,1,0:T(8,128)} %image_hbm.1), custom_call_target="tpu_custom_call" | custom-call | flops 99999997952 | bytes 6291456 | tf_op jit(solution)/shard_map/match/pallas_call | solution.py:157
  8.1 6.6 %warp_meta.1 = (f32[8,184,128]{2,1,0:T(8,128)S(1)}, f32[8,184,128]{2,1,0:T(8,128)S(1)}, f32[8,160,128]{2,1,0:T(8,128)S(1)}, f32[8,160,128]{2,1,0:T(8,128)S(1)}, ...) custom-call(f32[16,128]{1,0:T(8,128)S(1)} %copy-done, ...), custom_call_target="tpu_custom_call" | custom-call | flops 10000000000 | bytes 8388608 | tf_op jit(solution)/shard_map/warp_meta/pallas_call | solution.py:298
  14.7 4.2 %collective-permute-start.6 = (f32[8,160,128]{2,1,0:T(8,128)S(1)}, f32[8,160,128]{2,1,0:T(8,128)S(1)}, u32[]{:S(2)}, u32[]{:S(2)}) collective-permute-start(f32[8,160,128]{2,1,0:T(8,128)S(1)} %get-tuple-element.37), channel_id=1, source_target_pairs={{8,16},{3,5},{10,18},{11,13},{12,20},{19,21},{14,22},{27,29},{16,8... | collective-permute-start | bytes 1966088 | tf_op jit(solution)/shard_map/ppermute | solution.py:389
  18.9 1.5 %collective-permute-start.7 = (f32[2,16,48,128]{3,2,1,0:T(8,128)S(1)}, f32[2,16,48,128]{3,2,1,0:T(8,128)S(1)}, u32[]{:S(2)}, u32[]{:S(2)}) collective-permute-start(f32[2,16,48,128]{3,2,1,0:T(8,128)S(1)} %get-tuple-element.39), channel_id=1, source_target_pairs={{0,32},{2,34},{4,36},{6,38},{8,40},{10,42},{12,44},{14,46},{16,48}... | collective-permute-start | bytes 2359304 | tf_op jit(solution)/shard_map/ppermute | solution.py:392
  20.4 4.9 %warp.1 = (f32[8,256,128]{2,1,0:T(8,128)S(1)}, f32[8,256,128]{2,1,0:T(8,128)S(1)}, f32[8,256,128]{2,1,0:T(8,128)S(1)}, f32[8,256,128]{2,1,0:T(8,128)S(1)}) custom-call(s32[2,128]{1,0:T(2,128)S(1)} %get-tuple-element.28.refs_0_, f32[16,128]{1,0:T(8,128)S(1)} %copy-done, f32[16,128]{1,0:T(8,128)S(1)} %collective-permute-done.refs_1_.refs_2_, ...), custom_call_target="tpu_custom_call" | custom-call | flops 10000000000 | bytes 8388608 | tf_op jit(solution)/shard_map/warp/pallas_call | solution.py:298
  25.3 2.1 %collective-permute-start.3 = (f32[8,256,128]{2,1,0:T(8,128)S(1)}, f32[8,256,128]{2,1,0:T(8,128)S(1)}, u32[]{:S(2)}, u32[]{:S(2)}) collective-permute-start(f32[8,256,128]{2,1,0:T(8,128)S(1)} %get-tuple-element.32), channel_id=1, source_target_pairs={{0,8},{1,3},{2,10},{9,11},{4,12},{17,19},{6,14},{25,27},{8,0},{3,1... | collective-permute-start | bytes 3145736 | tf_op jit(solution)/shard_map/ppermute | solution.py:389
  27.5 3.4 %collective-permute-done.7 = f32[2,16,48,128]{3,2,1,0:T(8,128)S(1)} collective-permute-done((f32[2,16,48,128]{3,2,1,0:T(8,128)S(1)}, f32[2,16,48,128]{3,2,1,0:T(8,128)S(1)}, u32[]{:S(2)}, u32[]{:S(2)}) %collective-permute-start.7) | collective-permute-done | bytes 786464 | tf_op jit(solution)/shard_map/ppermute | solution.py:392
  31.0 2.8 %collective-permute-start.10 = (f32[16,48,128]{2,1,0:T(8,128)S(1)}, f32[16,48,128]{2,1,0:T(8,128)S(1)}, u32[]{:S(2)}, u32[]{:S(2)}) collective-permute-start(f32[16,48,128]{2,1,0:T(8,128)S(1)} %get-tuple-element.57), channel_id=1, source_target_pairs={{32,64},{34,66},{36,68},{38,70},{40,72},{42,74},{44,76},{46,78},{4... | collective-permute-start | bytes 1179656 | tf_op jit(solution)/shard_map/ppermute | solution.py:392
  33.9 2.1 %collective-permute-start.14 = (f32[4,160,128]{2,1,0:T(8,128)S(1)}, f32[4,160,128]{2,1,0:T(8,128)S(1)}, u32[]{:S(2)}, u32[]{:S(2)}) collective-permute-start(f32[4,160,128]{2,1,0:T(8,128)S(1)} %get-tuple-element.61), channel_id=1, source_target_pairs={{0,8},{1,3},{2,10},{9,11},{4,12},{17,19},{6,14},{25,27},{8,0},{3,1... | collective-permute-start | bytes 983048 | tf_op jit(solution)/shard_map/ppermute | solution.py:389
  36.3 3.7 %collective-permute-done.10 = f32[16,48,128]{2,1,0:T(8,128)S(1)} collective-permute-done((f32[16,48,128]{2,1,0:T(8,128)S(1)}, f32[16,48,128]{2,1,0:T(8,128)S(1)}, u32[]{:S(2)}, u32[]{:S(2)}) %collective-permute-start.10) | collective-permute-done | bytes 393248 | tf_op jit(solution)/shard_map/ppermute | solution.py:392
  40.1 2.1 %collective-permute-start.11 = (f32[8,48,128]{2,1,0:T(8,128)S(1)}, f32[8,48,128]{2,1,0:T(8,128)S(1)}, u32[]{:S(2)}, u32[]{:S(2)}) collective-permute-start(f32[8,48,128]{2,1,0:T(8,128)S(1)} %get-tuple-element.67), channel_id=1, source_target_pairs={{0,8},{1,3},{2,10},{9,11},{4,12},{17,19},{6,14},{25,27},{8,0},{3,1... | collective-permute-start | bytes 589832 | tf_op jit(solution)/shard_map/ppermute | solution.py:389
  42.2 1.3 %collective-permute-done.4 = f32[8,256,128]{2,1,0:T(8,128)S(1)} collective-permute-done((f32[8,256,128]{2,1,0:T(8,128)S(1)}, f32[8,256,128]{2,1,0:T(8,128)S(1)}, u32[]{:S(2)}, u32[]{:S(2)}) %collective-permute-start.4) | collective-permute-done | bytes 1048608 | tf_op jit(solution)/shard_map/ppermute | solution.py:389
  44.1 3.3 %collective-permute-done.11 = f32[8,48,128]{2,1,0:T(8,128)S(1)} collective-permute-done((f32[8,48,128]{2,1,0:T(8,128)S(1)}, f32[8,48,128]{2,1,0:T(8,128)S(1)}, u32[]{:S(2)}, u32[]{:S(2)}) %collective-permute-start.11) | collective-permute-done | bytes 196640 | tf_op jit(solution)/shard_map/ppermute | solution.py:389
  47.7 5.4 %collective-permute-done.9 = f32[4,256,128]{2,1,0:T(8,128)S(1)} collective-permute-done((f32[4,256,128]{2,1,0:T(8,128)S(1)}, f32[4,256,128]{2,1,0:T(8,128)S(1)}, u32[]{:S(2)}, u32[]{:S(2)}) %collective-permute-start.9) | collective-permute-done | bytes 524320 | tf_op jit(solution)/shard_map/ppermute | solution.py:389
  53.0 1.4 %collective-permute-done.8 = f32[4,256,128]{2,1,0:T(8,128)S(1)} collective-permute-done((f32[4,256,128]{2,1,0:T(8,128)S(1)}, f32[4,256,128]{2,1,0:T(8,128)S(1)}, u32[]{:S(2)}, u32[]{:S(2)}) %collective-permute-start.8) | collective-permute-done | bytes 524320 | tf_op jit(solution)/shard_map/ppermute | solution.py:389
  54.6 3.1 %collective-permute-start.12 = (f32[2,512,128]{2,1,0:T(8,128)S(1)}, f32[2,512,128]{2,1,0:T(8,128)S(1)}, u32[]{:S(2)}, u32[]{:S(2)}) collective-permute-start(f32[2,512,128]{2,1,0:T(8,128)S(1)} %pad_maximum_fusion), channel_id=1, source_target_pairs={{2,4},{9,17},{10,12},{11,19},{18,20},{13,21},{26,28},{15,23},{4,2}... | collective-permute-start | bytes 1572872 | tf_op jit(solution)/shard_map/ppermute | solution.py:389
  58.0 7.1 %collective-permute-done.12 = f32[2,512,128]{2,1,0:T(8,128)S(1)} collective-permute-done((f32[2,512,128]{2,1,0:T(8,128)S(1)}, f32[2,512,128]{2,1,0:T(8,128)S(1)}, u32[]{:S(2)}, u32[]{:S(2)}) %collective-permute-start.12) | collective-permute-done | bytes 524320 | tf_op jit(solution)/shard_map/ppermute | solution.py:389
  65.8 2.6 %collective-permute-start.20 = (f32[1,392,128]{2,1,0:T(8,128)S(1)}, f32[1,392,128]{2,1,0:T(8,128)S(1)}, u32[]{:S(2)}, u32[]{:S(2)}) collective-permute-start(f32[1,392,128]{2,1,0:T(8,128)S(1)} %slice_add_fusion.14), channel_id=1, source_target_pairs={{2,4},{9,17},{10,12},{11,19},{18,20},{13,21},{26,28},{15,23},{4,2}... | collective-permute-start | bytes 602120 | tf_op jit(solution)/shard_map/ppermute | solution.py:389
  68.4 3.2 %collective-permute-done.16 = f32[1,512,128]{2,1,0:T(8,128)S(1)} collective-permute-done((f32[1,512,128]{2,1,0:T(8,128)S(1)}, f32[1,512,128]{2,1,0:T(8,128)S(1)}, u32[]{:S(2)}, u32[]{:S(2)}) %collective-permute-start.16) | collective-permute-done | bytes 262176 | tf_op jit(solution)/shard_map/ppermute | solution.py:389
  72.8 2.3 %collective-permute-start.21 = (f32[392,128]{1,0:T(8,128)S(1)}, f32[392,128]{1,0:T(8,128)S(1)}, u32[]{:S(2)}, u32[]{:S(2)}) collective-permute-start(f32[392,128]{1,0:T(8,128)S(1)} %bitcast.24), channel_id=1, source_target_pairs={{32,64},{34,66},{36,68},{38,70},{40,72},{42,74},{44,76},{46,78},{4... | collective-permute-start | bytes 602120 | tf_op jit(solution)/shard_map/ppermute | solution.py:392
  75.2 6.0 %collective-permute-done.21 = f32[392,128]{1,0:T(8,128)S(1)} collective-permute-done((f32[392,128]{1,0:T(8,128)S(1)}, f32[392,128]{1,0:T(8,128)S(1)}, u32[]{:S(2)}, u32[]{:S(2)}) %collective-permute-start.21) | collective-permute-done | bytes 200736 | tf_op jit(solution)/shard_map/ppermute | solution.py:392
  81.6 2.8 %collective-permute-start.18 = (f32[512,128]{1,0:T(8,128)S(1)}, f32[512,128]{1,0:T(8,128)S(1)}, u32[]{:S(2)}, u32[]{:S(2)}) collective-permute-start(f32[512,128]{1,0:T(8,128)S(1)} %add.129.num), channel_id=1, source_target_pairs={{32,64},{34,66},{36,68},{38,70},{40,72},{42,74},{44,76},{46,78},{4... | collective-permute-start | bytes 786440 | tf_op jit(solution)/shard_map/ppermute | solution.py:392
  84.5 2.9 %collective-permute-done.22.got = f32[440,128]{1,0:T(8,128)S(1)} collective-permute-done((f32[440,128]{1,0:T(8,128)S(1)}, f32[440,128]{1,0:T(8,128)S(1)}, u32[]{:S(2)}, u32[]{:S(2)}) %collective-permute-start.22) | collective-permute-done | bytes 225312 | tf_op jit(solution)/shard_map/ppermute | solution.py:392
  (56 shorter events, 7.6 us)
Async XLA Ops:
  2.1 5.9 %collective-permute-start = (f32[16,128]{1,0:T(8,128)}, f32[16,128]{1,0:T(8,128)S(1)}, u32[]{:S(2)}, u32[]{:S(2)}) collective-permute-start(f32[16,128]{1,0:T(8,128)} %pack.1.refs_0_.refs_1_), channel_id=1, source_target_pairs={{0,1},{1,0},{2,3},{3,2},{4,5},{5,4},{6,7},{7,6},{8,9},{9,8},{10,11... | collective-permute-start | bytes 24584 | tf_op jit(solution)/shard_map/ppermute | solution.py:444
  2.1 6.0 %collective-permute-start.1 = (f32[32,128,128]{2,1,0:T(8,128)}, f32[32,128,128]{2,1,0:T(8,128)S(1)}, u32[]{:S(2)}, u32[]{:S(2)}) collective-permute-start(f32[32,128,128]{2,1,0:T(8,128)} %refs_2_.1), channel_id=1, source_target_pairs={{0,1},{1,0},{2,3},{3,2},{4,5},{5,4},{6,7},{7,6},{8,9},{9,8},{10,11... | collective-permute-start | bytes 6291464 | tf_op jit(solution)/shard_map/ppermute | solution.py:442
  2.6 5.5 %copy-start.1 = (f32[32,128,128]{2,1,0:T(8,128)S(1)}, f32[32,128,128]{2,1,0:T(8,128)}, u32[]{:S(2)}) copy-start(f32[32,128,128]{2,1,0:T(8,128)} %refs_2_.1) | copy-start | bytes 6291460
  7.9 12.4 %collective-permute-start.2 = (f32[4360,128]{1,0:T(8,128)S(1)}, f32[4360,128]{1,0:T(8,128)S(1)}, u32[]{:S(2)}, u32[]{:S(2)}) collective-permute-start(f32[4360,128]{1,0:T(8,128)S(1)} %match.1.refs_4_), channel_id=1, source_target_pairs={{0,1},{1,0},{2,3},{3,2},{4,5},{5,4},{6,7},{7,6},{8,9},{9,8},{10,11... | collective-permute-start | bytes 6696968 | tf_op jit(solution)/shard_map/ppermute | solution.py:447
  14.7 19.1 %collective-permute-start.6 = (f32[8,160,128]{2,1,0:T(8,128)S(1)}, f32[8,160,128]{2,1,0:T(8,128)S(1)}, u32[]{:S(2)}, u32[]{:S(2)}) collective-permute-start(f32[8,160,128]{2,1,0:T(8,128)S(1)} %get-tuple-element.37), channel_id=1, source_target_pairs={{8,16},{3,5},{10,18},{11,13},{12,20},{19,21},{14,22},{27,29},{16,8... | collective-permute-start | bytes 1966088 | tf_op jit(solution)/shard_map/ppermute | solution.py:389
  18.9 17.1 %collective-permute-start.5 = (f32[8,184,128]{2,1,0:T(8,128)S(1)}, f32[8,184,128]{2,1,0:T(8,128)S(1)}, u32[]{:S(2)}, u32[]{:S(2)}) collective-permute-start(f32[8,184,128]{2,1,0:T(8,128)S(1)} %get-tuple-element.35), channel_id=1, source_target_pairs={{0,8},{1,3},{2,10},{9,11},{4,12},{17,19},{6,14},{25,27},{8,0},{3,1... | collective-permute-start | bytes 2261000 | tf_op jit(solution)/shard_map/ppermute | solution.py:389
  18.9 12.0 %collective-permute-start.7 = (f32[2,16,48,128]{3,2,1,0:T(8,128)S(1)}, f32[2,16,48,128]{3,2,1,0:T(8,128)S(1)}, u32[]{:S(2)}, u32[]{:S(2)}) collective-permute-start(f32[2,16,48,128]{3,2,1,0:T(8,128)S(1)} %get-tuple-element.39), channel_id=1, source_target_pairs={{0,32},{2,34},{4,36},{6,38},{8,40},{10,42},{12,44},{14,46},{16,48}... | collective-permute-start | bytes 2359304 | tf_op jit(solution)/shard_map/ppermute | solution.py:392
  25.3 16.9 %collective-permute-start.3 = (f32[8,256,128]{2,1,0:T(8,128)S(1)}, f32[8,256,128]{2,1,0:T(8,128)S(1)}, u32[]{:S(2)}, u32[]{:S(2)}) collective-permute-start(f32[8,256,128]{2,1,0:T(8,128)S(1)} %get-tuple-element.32), channel_id=1, source_target_pairs={{0,8},{1,3},{2,10},{9,11},{4,12},{17,19},{6,14},{25,27},{8,0},{3,1... | collective-permute-start | bytes 3145736 | tf_op jit(solution)/shard_map/ppermute | solution.py:389
  27.5 16.0 %collective-permute-start.4 = (f32[8,256,128]{2,1,0:T(8,128)S(1)}, f32[8,256,128]{2,1,0:T(8,128)S(1)}, u32[]{:S(2)}, u32[]{:S(2)}) collective-permute-start(f32[8,256,128]{2,1,0:T(8,128)S(1)} %get-tuple-element.33), channel_id=1, source_target_pairs={{8,16},{3,5},{10,18},{11,13},{12,20},{19,21},{14,22},{27,29},{16,8... | collective-permute-start | bytes 3145736 | tf_op jit(solution)/shard_map/ppermute | solution.py:389
  31.0 9.1 %collective-permute-start.10 = (f32[16,48,128]{2,1,0:T(8,128)S(1)}, f32[16,48,128]{2,1,0:T(8,128)S(1)}, u32[]{:S(2)}, u32[]{:S(2)}) collective-permute-start(f32[16,48,128]{2,1,0:T(8,128)S(1)} %get-tuple-element.57), channel_id=1, source_target_pairs={{32,64},{34,66},{36,68},{38,70},{40,72},{42,74},{44,76},{46,78},{4... | collective-permute-start | bytes 1179656 | tf_op jit(solution)/shard_map/ppermute | solution.py:392
  33.9 13.7 %collective-permute-start.14 = (f32[4,160,128]{2,1,0:T(8,128)S(1)}, f32[4,160,128]{2,1,0:T(8,128)S(1)}, u32[]{:S(2)}, u32[]{:S(2)}) collective-permute-start(f32[4,160,128]{2,1,0:T(8,128)S(1)} %get-tuple-element.61), channel_id=1, source_target_pairs={{0,8},{1,3},{2,10},{9,11},{4,12},{17,19},{6,14},{25,27},{8,0},{3,1... | collective-permute-start | bytes 983048 | tf_op jit(solution)/shard_map/ppermute | solution.py:389
  36.2 11.4 %collective-permute-start.13 = (f32[4,184,128]{2,1,0:T(8,128)S(1)}, f32[4,184,128]{2,1,0:T(8,128)S(1)}, u32[]{:S(2)}, u32[]{:S(2)}) collective-permute-start(f32[4,184,128]{2,1,0:T(8,128)S(1)} %get-tuple-element.59), channel_id=1, source_target_pairs={{8,16},{3,5},{10,18},{11,13},{12,20},{19,21},{14,22},{27,29},{16,8... | collective-permute-start | bytes 1130504 | tf_op jit(solution)/shard_map/ppermute | solution.py:389
  40.1 7.3 %collective-permute-start.11 = (f32[8,48,128]{2,1,0:T(8,128)S(1)}, f32[8,48,128]{2,1,0:T(8,128)S(1)}, u32[]{:S(2)}, u32[]{:S(2)}) collective-permute-start(f32[8,48,128]{2,1,0:T(8,128)S(1)} %get-tuple-element.67), channel_id=1, source_target_pairs={{0,8},{1,3},{2,10},{9,11},{4,12},{17,19},{6,14},{25,27},{8,0},{3,1... | collective-permute-start | bytes 589832 | tf_op jit(solution)/shard_map/ppermute | solution.py:389
  43.6 9.4 %collective-permute-start.9 = (f32[4,256,128]{2,1,0:T(8,128)S(1)}, f32[4,256,128]{2,1,0:T(8,128)S(1)}, u32[]{:S(2)}, u32[]{:S(2)}) collective-permute-start(f32[4,256,128]{2,1,0:T(8,128)S(1)} %get-tuple-element.54), channel_id=1, source_target_pairs={{0,8},{1,3},{2,10},{9,11},{4,12},{17,19},{6,14},{25,27},{8,0},{3,1... | collective-permute-start | bytes 1572872 | tf_op jit(solution)/shard_map/ppermute | solution.py:389
  44.0 10.5 %collective-permute-start.8 = (f32[4,256,128]{2,1,0:T(8,128)S(1)}, f32[4,256,128]{2,1,0:T(8,128)S(1)}, u32[]{:S(2)}, u32[]{:S(2)}) collective-permute-start(f32[4,256,128]{2,1,0:T(8,128)S(1)} %get-tuple-element.53), channel_id=1, source_target_pairs={{8,16},{3,5},{10,18},{11,13},{12,20},{19,21},{14,22},{27,29},{16,8... | collective-permute-start | bytes 1572872 | tf_op jit(solution)/shard_map/ppermute | solution.py:389
  47.4 10.3 %collective-permute-start.15 = (f32[4,48,128]{2,1,0:T(8,128)S(1)}, f32[4,48,128]{2,1,0:T(8,128)S(1)}, u32[]{:S(2)}, u32[]{:S(2)}) collective-permute-start(f32[4,48,128]{2,1,0:T(8,128)S(1)} %slice_add_fusion.24), channel_id=1, source_target_pairs={{8,16},{3,5},{10,18},{11,13},{12,20},{19,21},{14,22},{27,29},{16,8... | collective-permute-start | bytes 294920 | tf_op jit(solution)/shard_map/ppermute | solution.py:389
  54.6 10.5 %collective-permute-start.12 = (f32[2,512,128]{2,1,0:T(8,128)S(1)}, f32[2,512,128]{2,1,0:T(8,128)S(1)}, u32[]{:S(2)}, u32[]{:S(2)}) collective-permute-start(f32[2,512,128]{2,1,0:T(8,128)S(1)} %pad_maximum_fusion), channel_id=1, source_target_pairs={{2,4},{9,17},{10,12},{11,19},{18,20},{13,21},{26,28},{15,23},{4,2}... | collective-permute-start | bytes 1572872 | tf_op jit(solution)/shard_map/ppermute | solution.py:389
  57.8 7.9 %collective-permute-start.19 = (f32[2,392,128]{2,1,0:T(8,128)S(1)}, f32[2,392,128]{2,1,0:T(8,128)S(1)}, u32[]{:S(2)}, u32[]{:S(2)}) collective-permute-start(f32[2,392,128]{2,1,0:T(8,128)S(1)} %pad_maximum_fusion.1), channel_id=1, source_target_pairs={{0,2},{1,9},{8,10},{3,11},{16,18},{5,13},{24,26},{7,15},{2,0},{9,1... | collective-permute-start | bytes 1204232 | tf_op jit(solution)/shard_map/ppermute | solution.py:389
  65.1 6.5 %collective-permute-start.16 = (f32[1,512,128]{2,1,0:T(8,128)S(1)}, f32[1,512,128]{2,1,0:T(8,128)S(1)}, u32[]{:S(2)}, u32[]{:S(2)}) collective-permute-start(f32[1,512,128]{2,1,0:T(8,128)S(1)} %fusion.5), channel_id=1, source_target_pairs={{0,2},{1,9},{8,10},{3,11},{16,18},{5,13},{24,26},{7,15},{2,0},{9,1... | collective-permute-start | bytes 786440 | tf_op jit(solution)/shard_map/ppermute | solution.py:389
  65.8 7.0 %collective-permute-start.20 = (f32[1,392,128]{2,1,0:T(8,128)S(1)}, f32[1,392,128]{2,1,0:T(8,128)S(1)}, u32[]{:S(2)}, u32[]{:S(2)}) collective-permute-start(f32[1,392,128]{2,1,0:T(8,128)S(1)} %slice_add_fusion.14), channel_id=1, source_target_pairs={{2,4},{9,17},{10,12},{11,19},{18,20},{13,21},{26,28},{15,23},{4,2}... | collective-permute-start | bytes 602120 | tf_op jit(solution)/shard_map/ppermute | solution.py:389
  71.6 10.0 %collective-permute-start.17 = (f32[512,128]{1,0:T(8,128)S(1)}, f32[512,128]{1,0:T(8,128)S(1)}, u32[]{:S(2)}, u32[]{:S(2)}) collective-permute-start(f32[512,128]{1,0:T(8,128)S(1)} %fusion.4), channel_id=1, source_target_pairs={{0,32},{2,34},{4,36},{6,38},{8,40},{10,42},{12,44},{14,46},{16,48}... | collective-permute-start | bytes 786440 | tf_op jit(solution)/shard_map/ppermute | solution.py:392
  72.8 8.4 %collective-permute-start.21 = (f32[392,128]{1,0:T(8,128)S(1)}, f32[392,128]{1,0:T(8,128)S(1)}, u32[]{:S(2)}, u32[]{:S(2)}) collective-permute-start(f32[392,128]{1,0:T(8,128)S(1)} %bitcast.24), channel_id=1, source_target_pairs={{32,64},{34,66},{36,68},{38,70},{40,72},{42,74},{44,76},{46,78},{4... | collective-permute-start | bytes 602120 | tf_op jit(solution)/shard_map/ppermute | solution.py:392
  81.3 6.1 %collective-permute-start.22 = (f32[440,128]{1,0:T(8,128)S(1)}, f32[440,128]{1,0:T(8,128)S(1)}, u32[]{:S(2)}, u32[]{:S(2)}) collective-permute-start(f32[440,128]{1,0:T(8,128)S(1)} %pad_maximum_fusion.4.var), channel_id=1, source_target_pairs={{0,32},{2,34},{4,36},{6,38},{8,40},{10,42},{12,44},{14,46},{16,48}... | collective-permute-start | bytes 675848 | tf_op jit(solution)/shard_map/ppermute | solution.py:392
  81.6 7.7 %collective-permute-start.18 = (f32[512,128]{1,0:T(8,128)S(1)}, f32[512,128]{1,0:T(8,128)S(1)}, u32[]{:S(2)}, u32[]{:S(2)}) collective-permute-start(f32[512,128]{1,0:T(8,128)S(1)} %add.129.num), channel_id=1, source_target_pairs={{32,64},{34,66},{36,68},{38,70},{40,72},{42,74},{44,76},{46,78},{4... | collective-permute-start | bytes 786440 | tf_op jit(solution)/shard_map/ppermute | solution.py:392
  (1 other events, 5.5 us)

commit v4 on v3

--- a/solution.py
+++ b/solution.py
@@ -25,8 +25,8 @@
 
 EMPTY = 1 << 24
 UNROLL = 12
-MATCH_UNROLL = 16
-CHUNKS = 2
+MATCH_UNROLL = 32
+CHUNKS = 1
 MATCH_COST = 100_000_000_000
 WARP_COST = 10_000_000_000
 

time: 90.2 us -> 90.2 us (level)
  no operation moved by 1% of the time
where the time goes in v4:
time: 90.2 us; the launch traced here: 90 us
  waiting for transfers between devices  38.9 us (43%)
  starting transfers between devices  28.8 us (32%)
  Pallas kernels  20.4 us (23%)
  other arithmetic  1.1 us (1%)
    ppermute x14, waiting for transfers between devices, cross(): return lax.ppermute(x, 'patch', over_patch(axis, edge))  22.2 us
    ppermute x14, starting transfers between devices, cross(): return lax.ppermute(x, 'patch', over_patch(axis, edge))  17.8 us
    ppermute x6, waiting for transfers between devices, visit(): return lax.ppermute(x, ('visit', 'patch'), over_visit(edge))  16.7 us
    pallas_call x2, Pallas kernels, warp(): pl.pallas_call(functools.partial(warp_kernel, with_meta), out_shape=outs,...  11.6 us
    ppermute x6, starting transfers between devices, visit(): return lax.ppermute(x, ('visit', 'patch'), over_visit(edge))  10.4 us
    pallas_call x1, Pallas kernels, match(): pl.pallas_call(match_kernel, out_shape=jax.ShapeDtypeStruct((TILES * PITC...  5.35 us
    pallas_call x2, Pallas kernels, finish(): pl.pallas_call(kernel, out_shape=[jax.ShapeDtypeStruct((PATCH, PATCH), F3...  2.01 us
  transfers between devices with their start and end apart: 23, of which 13 were waited for; matrix products, arithmetic and copies ran while one was open for 1% of the time, Pallas kernels for 20%

profile of v4, /device:TPU:0, one launch (start us, length us, event | category | flops | bytes accessed | tf_op | source)
XLA Modules:
  0.0 90.0 jit_solution(4292399407864270750)
XLA Ops:
  0.6 1.4 %pack.1.refs_0_.refs_1_ = f32[16,128]{1,0:T(8,128)} custom-call(s32[2,32]{1,0:T(2,128)} %bitcast.27, s32[2,2,32]{2,1,0:T(2,128)} %bitcast.25, f32[2,2,32]{2,1,0:T(2,128)} %bitcast.26), custom_call_target="tpu_custom_call" | custom-call | tf_op jit(solution)/shard_map/pack/pallas_call | solution.py:89
  2.6 5.3 %match.1.refs_4_ = f32[4360,128]{1,0:T(8,128)S(1)} custom-call(s32[3,32]{1,0:T(4,128)} %bitcast.28, f32[3,32]{1,0:T(4,128)} %bitcast.29, f32[8,2,41]{2,1,0:T(2,128)} %taps_hbm.1, f32[32,128,128]{2,1,0:T(8,128)} %image_hbm.1), custom_call_target="tpu_custom_call" | custom-call | flops 99999997952 | bytes 6291456 | tf_op jit(solution)/shard_map/match/pallas_call | solution.py:157
  8.1 6.6 %warp_meta.1 = (f32[8,184,128]{2,1,0:T(8,128)S(1)}, f32[8,184,128]{2,1,0:T(8,128)S(1)}, f32[8,160,128]{2,1,0:T(8,128)S(1)}, f32[8,160,128]{2,1,0:T(8,128)S(1)}, ...) custom-call(f32[16,128]{1,0:T(8,128)S(1)} %copy-done, ...), custom_call_target="tpu_custom_call" | custom-call | flops 10000000000 | bytes 8388608 | tf_op jit(solution)/shard_map/warp_meta/pallas_call | solution.py:298
  14.7 4.2 %collective-permute-start.6 = (f32[8,160,128]{2,1,0:T(8,128)S(1)}, f32[8,160,128]{2,1,0:T(8,128)S(1)}, u32[]{:S(2)}, u32[]{:S(2)}) collective-permute-start(f32[8,160,128]{2,1,0:T(8,128)S(1)} %get-tuple-element.37), channel_id=1, source_target_pairs={{8,16},{3,5},{10,18},{11,13},{12,20},{19,21},{14,22},{27,29},{16,8... | collective-permute-start | bytes 1966088 | tf_op jit(solution)/shard_map/ppermute | solution.py:389
  18.9 1.5 %collective-permute-start.7 = (f32[2,16,48,128]{3,2,1,0:T(8,128)S(1)}, f32[2,16,48,128]{3,2,1,0:T(8,128)S(1)}, u32[]{:S(2)}, u32[]{:S(2)}) collective-permute-start(f32[2,16,48,128]{3,2,1,0:T(8,128)S(1)} %get-tuple-element.39), channel_id=1, source_target_pairs={{0,32},{2,34},{4,36},{6,38},{8,40},{10,42},{12,44},{14,46},{16,48}... | collective-permute-start | bytes 2359304 | tf_op jit(solution)/shard_map/ppermute | solution.py:392
  20.4 5.0 %warp.1 = (f32[8,256,128]{2,1,0:T(8,128)S(1)}, f32[8,256,128]{2,1,0:T(8,128)S(1)}, f32[8,256,128]{2,1,0:T(8,128)S(1)}, f32[8,256,128]{2,1,0:T(8,128)S(1)}) custom-call(s32[2,128]{1,0:T(2,128)S(1)} %get-tuple-element.28.refs_0_, f32[16,128]{1,0:T(8,128)S(1)} %copy-done, f32[16,128]{1,0:T(8,128)S(1)} %collective-permute-done.refs_1_.refs_2_, ...), custom_call_target="tpu_custom_call" | custom-call | flops 10000000000 | bytes 8388608 | tf_op jit(solution)/shard_map/warp/pallas_call | solution.py:298
  25.4 2.1 %collective-permute-start.3 = (f32[8,256,128]{2,1,0:T(8,128)S(1)}, f32[8,256,128]{2,1,0:T(8,128)S(1)}, u32[]{:S(2)}, u32[]{:S(2)}) collective-permute-start(f32[8,256,128]{2,1,0:T(8,128)S(1)} %get-tuple-element.32), channel_id=1, source_target_pairs={{0,8},{1,3},{2,10},{9,11},{4,12},{17,19},{6,14},{25,27},{8,0},{3,1... | collective-permute-start | bytes 3145736 | tf_op jit(solution)/shard_map/ppermute | solution.py:389
  27.6 3.3 %collective-permute-done.7 = f32[2,16,48,128]{3,2,1,0:T(8,128)S(1)} collective-permute-done((f32[2,16,48,128]{3,2,1,0:T(8,128)S(1)}, f32[2,16,48,128]{3,2,1,0:T(8,128)S(1)}, u32[]{:S(2)}, u32[]{:S(2)}) %collective-permute-start.7) | collective-permute-done | bytes 786464 | tf_op jit(solution)/shard_map/ppermute | solution.py:392
  31.0 2.8 %collective-permute-start.10 = (f32[16,48,128]{2,1,0:T(8,128)S(1)}, f32[16,48,128]{2,1,0:T(8,128)S(1)}, u32[]{:S(2)}, u32[]{:S(2)}) collective-permute-start(f32[16,48,128]{2,1,0:T(8,128)S(1)} %get-tuple-element.57), channel_id=1, source_target_pairs={{32,64},{34,66},{36,68},{38,70},{40,72},{42,74},{44,76},{46,78},{4... | collective-permute-start | bytes 1179656 | tf_op jit(solution)/shard_map/ppermute | solution.py:392
  34.0 2.1 %collective-permute-start.14 = (f32[4,160,128]{2,1,0:T(8,128)S(1)}, f32[4,160,128]{2,1,0:T(8,128)S(1)}, u32[]{:S(2)}, u32[]{:S(2)}) collective-permute-start(f32[4,160,128]{2,1,0:T(8,128)S(1)} %get-tuple-element.61), channel_id=1, source_target_pairs={{0,8},{1,3},{2,10},{9,11},{4,12},{17,19},{6,14},{25,27},{8,0},{3,1... | collective-permute-start | bytes 983048 | tf_op jit(solution)/shard_map/ppermute | solution.py:389
  36.4 3.7 %collective-permute-done.10 = f32[16,48,128]{2,1,0:T(8,128)S(1)} collective-permute-done((f32[16,48,128]{2,1,0:T(8,128)S(1)}, f32[16,48,128]{2,1,0:T(8,128)S(1)}, u32[]{:S(2)}, u32[]{:S(2)}) %collective-permute-start.10) | collective-permute-done | bytes 393248 | tf_op jit(solution)/shard_map/ppermute | solution.py:392
  40.1 2.1 %collective-permute-start.11 = (f32[8,48,128]{2,1,0:T(8,128)S(1)}, f32[8,48,128]{2,1,0:T(8,128)S(1)}, u32[]{:S(2)}, u32[]{:S(2)}) collective-permute-start(f32[8,48,128]{2,1,0:T(8,128)S(1)} %get-tuple-element.67), channel_id=1, source_target_pairs={{0,8},{1,3},{2,10},{9,11},{4,12},{17,19},{6,14},{25,27},{8,0},{3,1... | collective-permute-start | bytes 589832 | tf_op jit(solution)/shard_map/ppermute | solution.py:389
  42.2 1.3 %collective-permute-done.4 = f32[8,256,128]{2,1,0:T(8,128)S(1)} collective-permute-done((f32[8,256,128]{2,1,0:T(8,128)S(1)}, f32[8,256,128]{2,1,0:T(8,128)S(1)}, u32[]{:S(2)}, u32[]{:S(2)}) %collective-permute-start.4) | collective-permute-done | bytes 1048608 | tf_op jit(solution)/shard_map/ppermute | solution.py:389
  44.2 3.2 %collective-permute-done.11 = f32[8,48,128]{2,1,0:T(8,128)S(1)} collective-permute-done((f32[8,48,128]{2,1,0:T(8,128)S(1)}, f32[8,48,128]{2,1,0:T(8,128)S(1)}, u32[]{:S(2)}, u32[]{:S(2)}) %collective-permute-start.11) | collective-permute-done | bytes 196640 | tf_op jit(solution)/shard_map/ppermute | solution.py:389
  47.7 5.3 %collective-permute-done.9 = f32[4,256,128]{2,1,0:T(8,128)S(1)} collective-permute-done((f32[4,256,128]{2,1,0:T(8,128)S(1)}, f32[4,256,128]{2,1,0:T(8,128)S(1)}, u32[]{:S(2)}, u32[]{:S(2)}) %collective-permute-start.9) | collective-permute-done | bytes 524320 | tf_op jit(solution)/shard_map/ppermute | solution.py:389
  53.1 1.4 %collective-permute-done.8 = f32[4,256,128]{2,1,0:T(8,128)S(1)} collective-permute-done((f32[4,256,128]{2,1,0:T(8,128)S(1)}, f32[4,256,128]{2,1,0:T(8,128)S(1)}, u32[]{:S(2)}, u32[]{:S(2)}) %collective-permute-start.8) | collective-permute-done | bytes 524320 | tf_op jit(solution)/shard_map/ppermute | solution.py:389
  54.6 3.1 %collective-permute-start.12 = (f32[2,512,128]{2,1,0:T(8,128)S(1)}, f32[2,512,128]{2,1,0:T(8,128)S(1)}, u32[]{:S(2)}, u32[]{:S(2)}) collective-permute-start(f32[2,512,128]{2,1,0:T(8,128)S(1)} %pad_maximum_fusion), channel_id=1, source_target_pairs={{2,4},{9,17},{10,12},{11,19},{18,20},{13,21},{26,28},{15,23},{4,2}... | collective-permute-start | bytes 1572872 | tf_op jit(solution)/shard_map/ppermute | solution.py:389
  58.1 7.0 %collective-permute-done.12 = f32[2,512,128]{2,1,0:T(8,128)S(1)} collective-permute-done((f32[2,512,128]{2,1,0:T(8,128)S(1)}, f32[2,512,128]{2,1,0:T(8,128)S(1)}, u32[]{:S(2)}, u32[]{:S(2)}) %collective-permute-start.12) | collective-permute-done | bytes 524320 | tf_op jit(solution)/shard_map/ppermute | solution.py:389
  65.8 2.6 %collective-permute-start.20 = (f32[1,392,128]{2,1,0:T(8,128)S(1)}, f32[1,392,128]{2,1,0:T(8,128)S(1)}, u32[]{:S(2)}, u32[]{:S(2)}) collective-permute-start(f32[1,392,128]{2,1,0:T(8,128)S(1)} %slice_add_fusion.14), channel_id=1, source_target_pairs={{2,4},{9,17},{10,12},{11,19},{18,20},{13,21},{26,28},{15,23},{4,2}... | collective-permute-start | bytes 602120 | tf_op jit(solution)/shard_map/ppermute | solution.py:389
  68.4 3.2 %collective-permute-done.16 = f32[1,512,128]{2,1,0:T(8,128)S(1)} collective-permute-done((f32[1,512,128]{2,1,0:T(8,128)S(1)}, f32[1,512,128]{2,1,0:T(8,128)S(1)}, u32[]{:S(2)}, u32[]{:S(2)}) %collective-permute-start.16) | collective-permute-done | bytes 262176 | tf_op jit(solution)/shard_map/ppermute | solution.py:389
  72.8 2.3 %collective-permute-start.21 = (f32[392,128]{1,0:T(8,128)S(1)}, f32[392,128]{1,0:T(8,128)S(1)}, u32[]{:S(2)}, u32[]{:S(2)}) collective-permute-start(f32[392,128]{1,0:T(8,128)S(1)} %bitcast.24), channel_id=1, source_target_pairs={{32,64},{34,66},{36,68},{38,70},{40,72},{42,74},{44,76},{46,78},{4... | collective-permute-start | bytes 602120 | tf_op jit(solution)/shard_map/ppermute | solution.py:392
  75.2 6.0 %collective-permute-done.21 = f32[392,128]{1,0:T(8,128)S(1)} collective-permute-done((f32[392,128]{1,0:T(8,128)S(1)}, f32[392,128]{1,0:T(8,128)S(1)}, u32[]{:S(2)}, u32[]{:S(2)}) %collective-permute-start.21) | collective-permute-done | bytes 200736 | tf_op jit(solution)/shard_map/ppermute | solution.py:392
  81.6 2.8 %collective-permute-start.18 = (f32[512,128]{1,0:T(8,128)S(1)}, f32[512,128]{1,0:T(8,128)S(1)}, u32[]{:S(2)}, u32[]{:S(2)}) collective-permute-start(f32[512,128]{1,0:T(8,128)S(1)} %add.129.num), channel_id=1, source_target_pairs={{32,64},{34,66},{36,68},{38,70},{40,72},{42,74},{44,76},{46,78},{4... | collective-permute-start | bytes 786440 | tf_op jit(solution)/shard_map/ppermute | solution.py:392
  84.4 2.9 %collective-permute-done.22.got = f32[440,128]{1,0:T(8,128)S(1)} collective-permute-done((f32[440,128]{1,0:T(8,128)S(1)}, f32[440,128]{1,0:T(8,128)S(1)}, u32[]{:S(2)}, u32[]{:S(2)}) %collective-permute-start.22) | collective-permute-done | bytes 225312 | tf_op jit(solution)/shard_map/ppermute | solution.py:392
  (56 shorter events, 7.7 us)
Async XLA Ops:
  2.1 5.9 %collective-permute-start = (f32[16,128]{1,0:T(8,128)}, f32[16,128]{1,0:T(8,128)S(1)}, u32[]{:S(2)}, u32[]{:S(2)}) collective-permute-start(f32[16,128]{1,0:T(8,128)} %pack.1.refs_0_.refs_1_), channel_id=1, source_target_pairs={{0,1},{1,0},{2,3},{3,2},{4,5},{5,4},{6,7},{7,6},{8,9},{9,8},{10,11... | collective-permute-start | bytes 24584 | tf_op jit(solution)/shard_map/ppermute | solution.py:444
  2.1 6.0 %collective-permute-start.1 = (f32[32,128,128]{2,1,0:T(8,128)}, f32[32,128,128]{2,1,0:T(8,128)S(1)}, u32[]{:S(2)}, u32[]{:S(2)}) collective-permute-start(f32[32,128,128]{2,1,0:T(8,128)} %refs_2_.1), channel_id=1, source_target_pairs={{0,1},{1,0},{2,3},{3,2},{4,5},{5,4},{6,7},{7,6},{8,9},{9,8},{10,11... | collective-permute-start | bytes 6291464 | tf_op jit(solution)/shard_map/ppermute | solution.py:442
  2.6 5.5 %copy-start.1 = (f32[32,128,128]{2,1,0:T(8,128)S(1)}, f32[32,128,128]{2,1,0:T(8,128)}, u32[]{:S(2)}) copy-start(f32[32,128,128]{2,1,0:T(8,128)} %refs_2_.1) | copy-start | bytes 6291460
  8.0 12.5 %collective-permute-start.2 = (f32[4360,128]{1,0:T(8,128)S(1)}, f32[4360,128]{1,0:T(8,128)S(1)}, u32[]{:S(2)}, u32[]{:S(2)}) collective-permute-start(f32[4360,128]{1,0:T(8,128)S(1)} %match.1.refs_4_), channel_id=1, source_target_pairs={{0,1},{1,0},{2,3},{3,2},{4,5},{5,4},{6,7},{7,6},{8,9},{9,8},{10,11... | collective-permute-start | bytes 6696968 | tf_op jit(solution)/shard_map/ppermute | solution.py:447
  14.7 19.2 %collective-permute-start.6 = (f32[8,160,128]{2,1,0:T(8,128)S(1)}, f32[8,160,128]{2,1,0:T(8,128)S(1)}, u32[]{:S(2)}, u32[]{:S(2)}) collective-permute-start(f32[8,160,128]{2,1,0:T(8,128)S(1)} %get-tuple-element.37), channel_id=1, source_target_pairs={{8,16},{3,5},{10,18},{11,13},{12,20},{19,21},{14,22},{27,29},{16,8... | collective-permute-start | bytes 1966088 | tf_op jit(solution)/shard_map/ppermute | solution.py:389
  18.9 17.1 %collective-permute-start.5 = (f32[8,184,128]{2,1,0:T(8,128)S(1)}, f32[8,184,128]{2,1,0:T(8,128)S(1)}, u32[]{:S(2)}, u32[]{:S(2)}) collective-permute-start(f32[8,184,128]{2,1,0:T(8,128)S(1)} %get-tuple-element.35), channel_id=1, source_target_pairs={{0,8},{1,3},{2,10},{9,11},{4,12},{17,19},{6,14},{25,27},{8,0},{3,1... | collective-permute-start | bytes 2261000 | tf_op jit(solution)/shard_map/ppermute | solution.py:389
  18.9 12.0 %collective-permute-start.7 = (f32[2,16,48,128]{3,2,1,0:T(8,128)S(1)}, f32[2,16,48,128]{3,2,1,0:T(8,128)S(1)}, u32[]{:S(2)}, u32[]{:S(2)}) collective-permute-start(f32[2,16,48,128]{3,2,1,0:T(8,128)S(1)} %get-tuple-element.39), channel_id=1, source_target_pairs={{0,32},{2,34},{4,36},{6,38},{8,40},{10,42},{12,44},{14,46},{16,48}... | collective-permute-start | bytes 2359304 | tf_op jit(solution)/shard_map/ppermute | solution.py:392
  25.4 16.8 %collective-permute-start.3 = (f32[8,256,128]{2,1,0:T(8,128)S(1)}, f32[8,256,128]{2,1,0:T(8,128)S(1)}, u32[]{:S(2)}, u32[]{:S(2)}) collective-permute-start(f32[8,256,128]{2,1,0:T(8,128)S(1)} %get-tuple-element.32), channel_id=1, source_target_pairs={{0,8},{1,3},{2,10},{9,11},{4,12},{17,19},{6,14},{25,27},{8,0},{3,1... | collective-permute-start | bytes 3145736 | tf_op jit(solution)/shard_map/ppermute | solution.py:389
  27.5 16.0 %collective-permute-start.4 = (f32[8,256,128]{2,1,0:T(8,128)S(1)}, f32[8,256,128]{2,1,0:T(8,128)S(1)}, u32[]{:S(2)}, u32[]{:S(2)}) collective-permute-start(f32[8,256,128]{2,1,0:T(8,128)S(1)} %get-tuple-element.33), channel_id=1, source_target_pairs={{8,16},{3,5},{10,18},{11,13},{12,20},{19,21},{14,22},{27,29},{16,8... | collective-permute-start | bytes 3145736 | tf_op jit(solution)/shard_map/ppermute | solution.py:389
  31.0 9.1 %collective-permute-start.10 = (f32[16,48,128]{2,1,0:T(8,128)S(1)}, f32[16,48,128]{2,1,0:T(8,128)S(1)}, u32[]{:S(2)}, u32[]{:S(2)}) collective-permute-start(f32[16,48,128]{2,1,0:T(8,128)S(1)} %get-tuple-element.57), channel_id=1, source_target_pairs={{32,64},{34,66},{36,68},{38,70},{40,72},{42,74},{44,76},{46,78},{4... | collective-permute-start | bytes 1179656 | tf_op jit(solution)/shard_map/ppermute | solution.py:392
  34.0 13.7 %collective-permute-start.14 = (f32[4,160,128]{2,1,0:T(8,128)S(1)}, f32[4,160,128]{2,1,0:T(8,128)S(1)}, u32[]{:S(2)}, u32[]{:S(2)}) collective-permute-start(f32[4,160,128]{2,1,0:T(8,128)S(1)} %get-tuple-element.61), channel_id=1, source_target_pairs={{0,8},{1,3},{2,10},{9,11},{4,12},{17,19},{6,14},{25,27},{8,0},{3,1... | collective-permute-start | bytes 983048 | tf_op jit(solution)/shard_map/ppermute | solution.py:389
  36.2 11.4 %collective-permute-start.13 = (f32[4,184,128]{2,1,0:T(8,128)S(1)}, f32[4,184,128]{2,1,0:T(8,128)S(1)}, u32[]{:S(2)}, u32[]{:S(2)}) collective-permute-start(f32[4,184,128]{2,1,0:T(8,128)S(1)} %get-tuple-element.59), channel_id=1, source_target_pairs={{8,16},{3,5},{10,18},{11,13},{12,20},{19,21},{14,22},{27,29},{16,8... | collective-permute-start | bytes 1130504 | tf_op jit(solution)/shard_map/ppermute | solution.py:389
  40.1 7.3 %collective-permute-start.11 = (f32[8,48,128]{2,1,0:T(8,128)S(1)}, f32[8,48,128]{2,1,0:T(8,128)S(1)}, u32[]{:S(2)}, u32[]{:S(2)}) collective-permute-start(f32[8,48,128]{2,1,0:T(8,128)S(1)} %get-tuple-element.67), channel_id=1, source_target_pairs={{0,8},{1,3},{2,10},{9,11},{4,12},{17,19},{6,14},{25,27},{8,0},{3,1... | collective-permute-start | bytes 589832 | tf_op jit(solution)/shard_map/ppermute | solution.py:389
  43.6 9.4 %collective-permute-start.9 = (f32[4,256,128]{2,1,0:T(8,128)S(1)}, f32[4,256,128]{2,1,0:T(8,128)S(1)}, u32[]{:S(2)}, u32[]{:S(2)}) collective-permute-start(f32[4,256,128]{2,1,0:T(8,128)S(1)} %get-tuple-element.54), channel_id=1, source_target_pairs={{0,8},{1,3},{2,10},{9,11},{4,12},{17,19},{6,14},{25,27},{8,0},{3,1... | collective-permute-start | bytes 1572872 | tf_op jit(solution)/shard_map/ppermute | solution.py:389
  44.0 10.5 %collective-permute-start.8 = (f32[4,256,128]{2,1,0:T(8,128)S(1)}, f32[4,256,128]{2,1,0:T(8,128)S(1)}, u32[]{:S(2)}, u32[]{:S(2)}) collective-permute-start(f32[4,256,128]{2,1,0:T(8,128)S(1)} %get-tuple-element.53), channel_id=1, source_target_pairs={{8,16},{3,5},{10,18},{11,13},{12,20},{19,21},{14,22},{27,29},{16,8... | collective-permute-start | bytes 1572872 | tf_op jit(solution)/shard_map/ppermute | solution.py:389
  47.5 10.3 %collective-permute-start.15 = (f32[4,48,128]{2,1,0:T(8,128)S(1)}, f32[4,48,128]{2,1,0:T(8,128)S(1)}, u32[]{:S(2)}, u32[]{:S(2)}) collective-permute-start(f32[4,48,128]{2,1,0:T(8,128)S(1)} %slice_add_fusion.24), channel_id=1, source_target_pairs={{8,16},{3,5},{10,18},{11,13},{12,20},{19,21},{14,22},{27,29},{16,8... | collective-permute-start | bytes 294920 | tf_op jit(solution)/shard_map/ppermute | solution.py:389
  54.6 10.5 %collective-permute-start.12 = (f32[2,512,128]{2,1,0:T(8,128)S(1)}, f32[2,512,128]{2,1,0:T(8,128)S(1)}, u32[]{:S(2)}, u32[]{:S(2)}) collective-permute-start(f32[2,512,128]{2,1,0:T(8,128)S(1)} %pad_maximum_fusion), channel_id=1, source_target_pairs={{2,4},{9,17},{10,12},{11,19},{18,20},{13,21},{26,28},{15,23},{4,2}... | collective-permute-start | bytes 1572872 | tf_op jit(solution)/shard_map/ppermute | solution.py:389
  57.8 7.9 %collective-permute-start.19 = (f32[2,392,128]{2,1,0:T(8,128)S(1)}, f32[2,392,128]{2,1,0:T(8,128)S(1)}, u32[]{:S(2)}, u32[]{:S(2)}) collective-permute-start(f32[2,392,128]{2,1,0:T(8,128)S(1)} %pad_maximum_fusion.1), channel_id=1, source_target_pairs={{0,2},{1,9},{8,10},{3,11},{16,18},{5,13},{24,26},{7,15},{2,0},{9,1... | collective-permute-start | bytes 1204232 | tf_op jit(solution)/shard_map/ppermute | solution.py:389
  65.1 6.5 %collective-permute-start.16 = (f32[1,512,128]{2,1,0:T(8,128)S(1)}, f32[1,512,128]{2,1,0:T(8,128)S(1)}, u32[]{:S(2)}, u32[]{:S(2)}) collective-permute-start(f32[1,512,128]{2,1,0:T(8,128)S(1)} %fusion.5), channel_id=1, source_target_pairs={{0,2},{1,9},{8,10},{3,11},{16,18},{5,13},{24,26},{7,15},{2,0},{9,1... | collective-permute-start | bytes 786440 | tf_op jit(solution)/shard_map/ppermute | solution.py:389
  65.8 7.0 %collective-permute-start.20 = (f32[1,392,128]{2,1,0:T(8,128)S(1)}, f32[1,392,128]{2,1,0:T(8,128)S(1)}, u32[]{:S(2)}, u32[]{:S(2)}) collective-permute-start(f32[1,392,128]{2,1,0:T(8,128)S(1)} %slice_add_fusion.14), channel_id=1, source_target_pairs={{2,4},{9,17},{10,12},{11,19},{18,20},{13,21},{26,28},{15,23},{4,2}... | collective-permute-start | bytes 602120 | tf_op jit(solution)/shard_map/ppermute | solution.py:389
  71.7 9.9 %collective-permute-start.17 = (f32[512,128]{1,0:T(8,128)S(1)}, f32[512,128]{1,0:T(8,128)S(1)}, u32[]{:S(2)}, u32[]{:S(2)}) collective-permute-start(f32[512,128]{1,0:T(8,128)S(1)} %fusion.4), channel_id=1, source_target_pairs={{0,32},{2,34},{4,36},{6,38},{8,40},{10,42},{12,44},{14,46},{16,48}... | collective-permute-start | bytes 786440 | tf_op jit(solution)/shard_map/ppermute | solution.py:392
  72.8 8.3 %collective-permute-start.21 = (f32[392,128]{1,0:T(8,128)S(1)}, f32[392,128]{1,0:T(8,128)S(1)}, u32[]{:S(2)}, u32[]{:S(2)}) collective-permute-start(f32[392,128]{1,0:T(8,128)S(1)} %bitcast.24), channel_id=1, source_target_pairs={{32,64},{34,66},{36,68},{38,70},{40,72},{42,74},{44,76},{46,78},{4... | collective-permute-start | bytes 602120 | tf_op jit(solution)/shard_map/ppermute | solution.py:392
  81.2 6.1 %collective-permute-start.22 = (f32[440,128]{1,0:T(8,128)S(1)}, f32[440,128]{1,0:T(8,128)S(1)}, u32[]{:S(2)}, u32[]{:S(2)}) collective-permute-start(f32[440,128]{1,0:T(8,128)S(1)} %pad_maximum_fusion.4.var), channel_id=1, source_target_pairs={{0,32},{2,34},{4,36},{6,38},{8,40},{10,42},{12,44},{14,46},{16,48}... | collective-permute-start | bytes 675848 | tf_op jit(solution)/shard_map/ppermute | solution.py:392
  81.6 7.7 %collective-permute-start.18 = (f32[512,128]{1,0:T(8,128)S(1)}, f32[512,128]{1,0:T(8,128)S(1)}, u32[]{:S(2)}, u32[]{:S(2)}) collective-permute-start(f32[512,128]{1,0:T(8,128)S(1)} %add.129.num), channel_id=1, source_target_pairs={{32,64},{34,66},{36,68},{38,70},{40,72},{42,74},{44,76},{46,78},{4... | collective-permute-start | bytes 786440 | tf_op jit(solution)/shard_map/ppermute | solution.py:392
  (1 other events, 5.5 us)
